TPU v7x, 32 devices: a whole 2x2x4 slice. The times are simulated.
32 devices in a mesh: dp: 8 (over z, x), tensor: 4 (over y, core).
Axes of the slice: x: 2, y: 2, z: 4, core: 2. Of those that a mesh axis runs over, the one named last changes fastest.
Arguments:
- x_in: bfloat16 [20480, 768], P(('dp', 'tensor')), may hold values from -6 to 6
- tags: int32 [128], P('dp'), may hold values from 0 to 1, as said below
- lengths: int32 [128], P('dp'), may hold values from 95 to 160, as said below
- w_qkv: bfloat16 [2, 768, 3, 768], P(None, 'dp', None, 'tensor'), may hold values from -0.3125 to 0.3125
- w_out: bfloat16 [2, 768, 768], P(None, 'dp', 'tensor'), may hold values from -1.5 to 1.5
- w_up: bfloat16 [2, 768, 3072], P(None, 'dp', 'tensor'), may hold values from -0.21875 to 0.21875
- w_down: bfloat16 [2, 768, 3072], P(None, 'dp', 'tensor'), may hold values from -0.109375 to 0.109375
- norm_gain: float32 [2, 2, 768], P(None, None, ('dp', 'tensor')), may hold values from 0.5 to 1.5
- norm_bias: float32 [2, 2, 768], P(None, None, ('dp', 'tensor')), may hold values from -2 to 2
- cotangent: bfloat16 [20480, 768], P(('dp', 'tensor')), may hold values from -6 to 6
Outputs:
- y_out: bfloat16 [20480, 768], P(('dp', 'tensor'))
- x_grad: float32 [20480, 768], P(('dp', 'tensor'))
- qkv_grad: float32 [2, 768, 3, 768], P(None, 'dp', None, 'tensor')
- out_grad: float32 [2, 768, 768], P(None, 'dp', 'tensor')
- up_grad: float32 [2, 768, 3072], P(None, 'dp', 'tensor')
- down_grad: float32 [2, 768, 3072], P(None, 'dp', 'tensor')
- gain_grad: float32 [2, 2, 768], P(None, None, ('dp', 'tensor'))
- bias_grad: float32 [2, 2, 768], P(None, None, ('dp', 'tensor'))
Inputs may be any that keep to these rules, and one draw needn't show every extreme that they name: `tags`: within the chains of each index of dp (a block of 16 in order), all heavy chains (0) come before all light ones (1); each block holds at least a quarter of either type. `lengths`: each device's chains (blocks of 4 in order) include one of length 160.
All inputs are finite; a program needn't handle non-finite values.
Results may differ from a plain program's by a relative error of at most 0.02.
Values may be sent and summed in bfloat16 or wider, within the bound.
A program may use at most 192 MiB of HBM per device.

v0:
```python
from functools import partial

import jax
import jax.numpy as jnp
from jax import lax
from jax.experimental import pallas as pl
from jax.experimental.pallas import tpu as pltpu
from jax.sharding import Mesh
from jax.sharding import PartitionSpec as P

D = 768
HEADS = 12
HEAD_DIM = 64
MICRO = 4
CHAINS_PART = 1
LENGTH = 160
GROUPS = 4
OWN = 4
EXTRA = 2
SLOTS = OWN + EXTRA
EXT_ROWS = EXTRA * LENGTH
OWN_ROWS = OWN * LENGTH
ROWS = SLOTS * LENGTH

EPS = 1e-12
NEG = -1e30
HIGH = lax.Precision.HIGHEST
BF = jnp.bfloat16
F32 = jnp.float32
MESH = pl.DeviceIdType.MESH
ANY = pl.BlockSpec(memory_space=pl.ANY)
AXES = ("z", "x", "y", "c")


def place():
    return tuple(lax.axis_index(a) for a in AXES)


def meet(nz, z, x, y, c):
    barrier = pltpu.get_barrier_semaphore()
    friends = [{"c": 1 - c}, {"y": 1 - y}, {"y": 1 - y, "c": 1 - c}, {"x": 1 - x}]
    friends += [{"z": lax.rem(z + dz, nz)} for dz in range(1, nz)]
    for friend in friends:
        pl.semaphore_signal(barrier, inc=1, device_id=friend, device_id_type=MESH)
    pl.semaphore_wait(barrier, len(friends))


CHUNK = 320
SUB = 80
N_CHUNK = ROWS // CHUNK
WIDE = 3 * LENGTH
GW = 256
PAIR = 3


def dot_nn(a, b):
    return lax.dot_general(a, b, (((1,), (0,)), ((), ())), preferred_element_type=F32)


def dot_nt(a, b):
    return lax.dot_general(a, b, (((1,), (1,)), ((), ())), preferred_element_type=F32)


def dot_tn(a, b):
    return lax.dot_general(a, b, (((0,), (0,)), ((), ())), preferred_element_type=F32)


def lanes(shape):
    return lax.broadcasted_iota(jnp.int32, shape, len(shape) - 1)


def head_mask(h, shape):
    lane = lanes(shape)
    return jnp.logical_and(lane >= h * HEAD_DIM, lane < (h + 1) * HEAD_DIM)


def stack_heads(rows):
    zero = jnp.zeros_like(rows)
    return jnp.concatenate([jnp.where(head_mask(h, rows.shape), rows, zero) for h in range(3)], 0)


def merge_heads(stack):
    out = jnp.zeros((LENGTH, GW), stack.dtype)
    for h in range(3):
        out = jnp.where(head_mask(h, out.shape), stack[h * LENGTH : (h + 1) * LENGTH], out)
    return out


def chunk_rows(i, size=CHUNK):
    return pl.ds(pl.multiple_of(i * size, size), size)


def loop(count, body):
    def step(i, carry):
        body(i)
        return carry

    lax.fori_loop(0, count, step, 0)


def weave(count, unit, extra):
    def body(i):
        unit(i)
        for k, step in extra.items():
            pl.when(i == k)(step)

    loop(count, body)


def out_columns(t, w, wo):
    low = lanes((D, 128)) < HEAD_DIM
    tiles = [w[0, t, :, GW * i + 128 : GW * i + 256].astype(F32) for i in range(3)]
    wo[t, :, :128] = jnp.where(low, pltpu.roll(tiles[0], 64, 1), tiles[1]).astype(BF)
    wo[t, :, 128:] = jnp.where(low, pltpu.roll(tiles[2], 64, 1), 0.0).astype(BF)


def attend(t, chains, lens, proj, probs, hout):
    rows = [chunk_rows(s, LENGTH) for s in chains]
    parts = [(proj[t, r, :GW], proj[t, r, GW : 2 * GW], proj[t, r, 2 * GW :]) for r in rows]
    lows, outs = [], []
    for s, (query, key, value) in zip(chains, parts):
        scores = dot_nt(key, stack_heads(query * jnp.asarray(0.125, BF)))
        valid = lax.broadcasted_iota(jnp.int32, (LENGTH, 1), 0) < lens(s)
        scores = jnp.where(valid, scores, NEG)
        expo = jnp.exp(scores - jnp.max(scores, 0, keepdims=True))
        lows.append((expo * (1.0 / jnp.sum(expo, 0, keepdims=True))).astype(BF))
        outs.append(merge_heads(dot_tn(lows[-1], value)).astype(BF))
    for s, r, low, out in zip(chains, rows, lows, outs):
        probs[t, s, :, :WIDE] = low
        hout[t, r] = out


def norm_rows(values):
    center = values - jnp.mean(values, -1, keepdims=True)
    factor = lax.rsqrt(jnp.mean(center * center, -1, keepdims=True) + EPS)
    return center * factor, factor


def norm_back(scaled, normed, factor):
    return factor * (
        scaled
        - jnp.mean(scaled, -1, keepdims=True)
        - normed * jnp.mean(scaled * normed, -1, keepdims=True)
    )


def pieces(i, body):
    def step(k):
        body(pl.ds(pl.multiple_of(i * CHUNK + k * SUB, SUB), SUB), k)

    loop(CHUNK // SUB, step)


def first_norm(i, x, hout, wo, prm, mid, n1, s1, mid_low):
    r = chunk_rows(i)
    attn = dot_nt(hout[0, r], wo[0])
    for t in range(1, GROUPS):
        attn += dot_nt(hout[t, r], wo[t])
    mid[r] = attn

    def piece(p, k):
        normed, factor = norm_rows(x[p].astype(F32) + mid[p])
        n1[p] = normed.astype(BF)
        s1[p] = jnp.broadcast_to(factor, (SUB, 128))
        value = normed * prm[0:1] + prm[2:3]
        mid[p] = value
        mid_low[p] = value.astype(BF)

    pieces(i, piece)


def feed_up(t, i, mid_low, w, act, slope):
    r = chunk_rows(i)
    for k in range(0, D, GW):
        up = dot_nn(mid_low[r], w[1, t, :, k : k + GW])
        cdf = 0.5 * (1.0 + lax.erf(up * 0.7071067811865476))
        act[t, r, k : k + GW] = (up * cdf).astype(BF)
        bell = 0.3989422804014327 * jnp.exp(-0.5 * up * up)
        slope[t, r, k : k + GW] = (cdf + up * bell).astype(BF)


def second_norm(i, act, w, prm, mid, cot, mine, y_rows, d_ffn, ngrad):
    r = chunk_rows(i)
    ffn = dot_nt(act[0, r], w[2, 0])
    for t in range(1, GROUPS):
        ffn += dot_nt(act[t, r], w[2, t])
    mid[r] += ffn

    def piece(p, k):
        normed, factor = norm_rows(mid[p])
        y_rows[pl.ds(pl.multiple_of(k * SUB, SUB), SUB)] = (normed * prm[1:2] + prm[3:4]).astype(BF)
        grad = cot[p].astype(F32) * jnp.where(k < LENGTH // SUB, mine(2 * i), mine(2 * i + 1))
        ngrad[1:2] += jnp.sum(grad * normed, 0, keepdims=True)
        ngrad[3:4] += jnp.sum(grad, 0, keepdims=True)
        back = norm_back(grad * prm[1:2], normed, factor)
        mid[p] = back
        d_ffn[p] = back.astype(BF)

    pieces(i, piece)


def back_up(t, i, d_ffn, w, slope):
    r = chunk_rows(i)
    slope[t, r] = (dot_nn(d_ffn[r], w[2, t]) * slope[t, r].astype(F32)).astype(BF)


def back_first_norm(i, d_up, w, prm, mid, n1, s1, d_attn, ngrad):
    r = chunk_rows(i)
    grad = dot_nt(d_up[0, r], w[1, 0])
    for t in range(1, GROUPS):
        grad += dot_nt(d_up[t, r], w[1, t])
    mid[r] += grad

    def piece(p, k):
        grad = mid[p]
        normed = n1[p].astype(F32)
        ngrad[0:1] += jnp.sum(grad * normed, 0, keepdims=True)
        ngrad[2:3] += jnp.sum(grad, 0, keepdims=True)
        back = norm_back(grad * prm[0:1], normed, s1[p, 0:1])
        mid[p] = back
        d_attn[p] = back.astype(BF)

    pieces(i, piece)


def back_heads(t, i, d_attn, wo, d_heads):
    r = chunk_rows(i)
    d_heads[t, r, :GW] = dot_nn(d_attn[r], wo[t]).astype(BF)


def back_attend(t, chains, proj, probs, d_heads):
    rows = [chunk_rows(s, LENGTH) for s in chains]
    parts = [
        (proj[t, r, :GW], proj[t, r, GW : 2 * GW], proj[t, r, 2 * GW :], d_heads[t, r, :GW], probs[t, s, :, :WIDE])
        for s, r in zip(chains, rows)
    ]
    results = []
    for query, key, value, grad, low in parts:
        grad = stack_heads(grad)
        p = low.astype(F32)
        d_probs = dot_nt(value, grad)
        d_scores = (p * (d_probs - jnp.sum(d_probs * p, 0, keepdims=True))).astype(BF)
        d_query = merge_heads(dot_tn(d_scores, key)) * 0.125
        d_key = dot_nn(d_scores, stack_heads(query * jnp.asarray(0.125, BF)))
        results.append((d_query.astype(BF), d_key.astype(BF), dot_nn(low, grad).astype(BF)))
    for r, (d_query, d_key, d_value) in zip(rows, results):
        proj[t, r, :GW] = d_query
        proj[t, r, GW : 2 * GW] = d_key
        proj[t, r, 2 * GW :] = d_value


def grad_qkv_out(t, x, d_proj, d_attn, hout, store):
    low = lanes((D, 128)) < HEAD_DIM
    outs = dot_tn(d_attn[...], hout[t])
    places = (pltpu.roll(outs[:, :128], 64, 1), outs[:, :128], pltpu.roll(outs[:, 128:], 64, 1))
    for i in range(3):
        part = dot_tn(x[...], d_proj[t, :, GW * i : GW * (i + 1)])
        store(GW * i, part[:, :128])
        store(GW * i + 128, jnp.where(low, part[:, 128:], places[i]))


def back_input(i, d_proj, w, mid, out):
    r = chunk_rows(i)
    grad = mid[r]
    for t in range(GROUPS):
        grad += dot_nt(d_proj[t, r], w[0, t])
    out(r, grad)


def remote(src, dst, s_sem, r_sem, who):
    return pltpu.make_async_remote_copy(
        src_ref=src, dst_ref=dst, send_sem=s_sem, recv_sem=r_sem, device_id=who, device_id_type=MESH
    )


def arrived(ref, sem):
    remote(ref, ref, sem, sem, {"c": 1 - lax.axis_index("c")}).wait_recv()


def has_left(ref, sem):
    remote(ref, ref, sem, sem, {"c": 1 - lax.axis_index("c")}).wait_send()


def step_kernel(nz, rows,
                tags, lens, x_in, cot, qo, up, dn, gain, bias,
                y_own, g_own, own_out, oth_out, n_out, y_back, g_back, r_c,
                w, x, proj, probs, hout, wo, mid, n1, s1, mid_low, act, slope, d_ffn, gown, r_x,
                n_all, prm, ngrad, n_c, n_x, n_z,
                load_s, io_s, stage_s,
                ys_s, ys_r, zs_s, zs_r, xs_s, xs_r, cs_s, cs_r, ex_s, ex_r, na_s, na_r,
                c_s, c_r, x_s, x_r, z_s, z_r, y_s, y_r, e_s, e_r, ng_s, ng_r, free_s):
    z, xc, y, c = place()
    core, across, other_x = {"c": 1 - c}, {"y": 1 - y}, {"x": 1 - xc}
    diagonal = {"y": 1 - y, "c": 1 - c}
    mats = (qo, up, dn)
    lender = y != c
    home = (2 * y + c) * OWN
    away = (2 - y) * OWN + c * EXTRA

    def z_of(dz):
        return lax.rem(z + dz, nz)

    def chain(s):
        return jnp.where(s < OWN, home + s, away + s - OWN)

    def length_of(s):
        return lens[chain(s)]

    def mine(s):
        return jnp.where(tags[chain(s)] == y, 1.0, 0.0)

    def part(zz, xx):
        return pl.ds(pl.multiple_of((zz * 2 + xx) * rows, rows), rows)

    def group(g):
        return 2 * lax.rem(y + g, 2) + c

    def block(m, g, zz, xx):
        return w.at[m, group(g), part(zz, xx)]

    loads = [pltpu.make_async_copy(mats[m].at[y], block(m, 0, z, xc), load_s.at[m]) for m in range(3)]
    loads += [
        pltpu.make_async_copy(x_in, x.at[pl.ds(0, OWN_ROWS)], load_s.at[3]),
        pltpu.make_async_copy(cot, d_ffn.at[pl.ds(0, OWN_ROWS)], load_s.at[4]),
    ]
    for cp in loads:
        cp.start()
    me = ((z * 2 + xc) * 2 + y) * 2 + c
    cols = gain.shape[2]
    n_all[me] = jnp.zeros((8, 128), F32)
    for i in range(2):
        n_all[me, 2 * i : 2 * i + 2, :cols] = gain[i]
        n_all[me, 4 + 2 * i : 6 + 2 * i, :cols] = bias[i]
    ngrad[...] = jnp.zeros_like(ngrad)
    meet(nz, z, xc, y, c)

    def lend(arr, out, i, act_on):
        @pl.when(lender)
        def _():
            for j, (who, p) in enumerate(((across, c), (diagonal, 1 - c))):
                src = arr.at[pl.ds(pl.multiple_of(p * EXT_ROWS, EXT_ROWS), EXT_ROWS)]
                act_on(remote(src, out.at[pl.ds(OWN_ROWS, EXT_ROWS)], ex_s.at[i, j], ex_r.at[i], who))

    for m in range(3):
        remote(mats[m].at[1 - y], w.at[m, group(0), part(z, xc)], ys_s.at[m], ys_r.at[m], across).start()
    lend(x_in, x, 0, lambda cp: cp.start())
    lend(cot, d_ffn, 1, lambda cp: cp.start())

    def inside(zz):
        return jnp.logical_and(zz >= 0, zz < nz)

    def start(cp):
        cp.start()

    def recv(cp):
        cp.wait_recv()

    def hop(m, g, d, j, ref, act_on):
        to = z + 1 - 2 * d

        @pl.when(jnp.logical_and(inside(to), j < nz))
        def _():
            act_on(remote(ref, ref, zs_s.at[m, g, d, j], zs_r.at[m, g, d, j], {"z": to}))

    def x_copy(m, g, zz):
        ref = block(m, g, zz, xc)
        return remote(ref, ref, xs_s.at[m, g, zz], xs_r.at[m, g, zz], other_x)

    def c_copy(m, g, zz, xx):
        ref = block(m, g, zz, xx)
        return remote(ref, ref, cs_s.at[m, g, zz, xx], cs_r.at[m, g, zz, xx], core)

    def own_z(m):
        def body(g):
            @pl.when(g == 1)
            def _():
                arrived(block(m, 1, z, xc), ys_r.at[m])

            for d in range(2):
                hop(m, g, d, 1, block(m, g, z, xc), start)

        loop(2, body)

    def own_xc(m):
        def body(g):
            x_copy(m, g, z).start()
            c_copy(m, g, z, xc).start()

        loop(2, body)

    def z_event(m, j):
        def body(q):
            g, d = q // 2, q % 2
            zz = z - j + 2 * j * d

            @pl.when(inside(zz))
            def _():
                ref = block(m, g, zz, xc)
                arrived(ref, zs_r.at[m, g, d, j])
                hop(m, g, d, j + 1, ref, start)
                x_copy(m, g, zz).start()
                c_copy(m, g, zz, xc).start()

        loop(4, body)

    def x_event(m, j):
        def body(q):
            g, d = q // 2, q % 2
            zz = z - j + 2 * j * d

            @pl.when(jnp.logical_and(inside(zz), j + 1 > d))
            def _():
                arrived(block(m, g, zz, 1 - xc), xs_r.at[m, g, zz])
                c_copy(m, g, zz, 1 - xc).start()

        loop(4, body)

    def gathered(m):
        def body(i):
            t = 2 * lax.rem(y + i // (2 * nz), 2) + 1 - c
            zz, xx = (i // 2) % nz, i % 2
            arrived(w.at[m, t, part(zz, xx)], cs_r.at[m, i // (2 * nz), zz, xx])

        loop(4 * nz, body)

    def gather_sent(i):
        m, g = i // 2, i % 2
        ref = w.at[0, 0, pl.ds(0, rows)]
        for j in range(1, nz):
            for d in range(2):
                @pl.when(inside(z - (1 - 2 * d) * (j - 1)))
                def _():
                    hop(m, g, d, j, ref, lambda cp: cp.wait_send())
        for zz in range(nz):
            has_left(ref, xs_s.at[m, g, zz])
            for xx in range(2):
                has_left(ref, cs_s.at[m, g, zz, xx])

    def norm_hop(i, act_on):
        if i == 0:
            act_on(remote(n_all.at[me], n_all.at[me], na_s.at[0], na_r.at[0], core))
        elif i == 1:
            ref = n_all.at[pl.ds(me - c, 2)]
            act_on(remote(ref, ref, na_s.at[1], na_r.at[1], across))
        elif i == 2:
            ref = n_all.at[pl.ds(me - c - 2 * y, 4)]
            act_on(remote(ref, ref, na_s.at[2], na_r.at[2], other_x))
        else:
            ref = n_all.at[pl.ds(8 * z, 8)]
            for dz in range(1, nz):
                act_on(remote(ref, ref, na_s.at[2 + dz], na_r.at[2 + dz], {"z": z_of(dz)}))

    for m in range(3):
        loads[m].wait()
    norm_hop(0, start)
    own_z(0)
    own_xc(0)
    z_event(0, 1)
    norm_hop(0, recv)
    norm_hop(1, start)
    for j in range(2, nz):
        z_event(0, j)
        if j == 2:
            own_z(1)
    if nz < 3:
        own_z(1)
    norm_hop(1, recv)
    norm_hop(2, start)
    own_xc(1)
    x_event(0, 0)
    x_event(0, 1)
    for j in range(1, nz - 1):
        z_event(1, j)
        x_event(0, j + 1)
    own_z(2)
    norm_hop(2, recv)
    norm_hop(3, start)
    gathered(0)
    loads[3].wait()
    arrived(x.at[pl.ds(OWN_ROWS, EXT_ROWS)], ex_r.at[0])

    def projection(i):
        t, k = i // N_CHUNK, i % N_CHUNK
        r = chunk_rows(k)
        proj[t, r] = dot_nn(x[r], w[0, t]).astype(BF)

        @pl.when(k == N_CHUNK - 1)
        def _():
            out_columns(t, w, wo)

    def more_own():
        z_event(1, nz - 1)
        own_xc(2)

    weave(
        GROUPS * N_CHUNK,
        projection,
        {0: more_own, 8: lambda: x_event(1, 0), 11: lambda: z_event(2, 1)},
    )
    norm_hop(3, recv)
    lane = lanes((2, D))
    gains, shifts = jnp.zeros((2, D), F32), jnp.zeros((2, D), F32)
    for d in range(8 * nz):
        within = jnp.logical_and(lane >= d * cols, lane < (d + 1) * cols)
        for name in range(2):
            piece = n_all[d, pl.ds(4 * name + 2 * y, 2), :]
            piece = jnp.concatenate([piece, jnp.zeros((2, D - 128), F32)], 1)
            piece = jnp.where(within, pltpu.roll(piece, d * cols, 1) if d else piece, 0.0)
            if name == 0:
                gains += piece
            else:
                shifts += piece
    prm[0:2] = gains
    prm[2:4] = shifts
    per = SLOTS // PAIR

    def attention(i):
        attend(i // per, [(i % per) * PAIR + k for k in range(PAIR)], length_of, proj, probs, hout)

    weave(
        GROUPS * per,
        attention,
        {2: lambda: x_event(1, 1), 3: lambda: z_event(2, 2), 7: lambda: x_event(1, 2)},
    )
    loop(N_CHUNK, lambda i: first_norm(i, x, hout, wo, prm, mid, n1, s1, mid_low))
    for j in range(3, nz):
        z_event(2, j)
        x_event(1, j)
    gathered(1)
    weave(
        GROUPS * N_CHUNK,
        lambda i: feed_up(i // N_CHUNK, i % N_CHUNK, mid_low, w, act, slope),
        {2: lambda: x_event(2, 0), 7: lambda: x_event(2, 1)},
    )
    for j in range(2, nz):
        x_event(2, j)
    gathered(2)
    loads[4].wait()
    arrived(d_ffn.at[pl.ds(OWN_ROWS, EXT_ROWS)], ex_r.at[1])

    def y_stage(i):
        return gown.at[1, i // 2, pl.ds(pl.multiple_of((i % 2) * CHUNK, CHUNK), CHUNK)]

    def give_back(src, dst, i, act_on):
        dst = dst.at[pl.ds(pl.multiple_of(c * EXT_ROWS, EXT_ROWS), EXT_ROWS)]

        @pl.when(c == y)
        def _():
            act_on(remote(src, dst, e_s.at[i], e_r.at[i, c], across))

        @pl.when(c != y)
        def _():
            act_on(remote(src, dst, e_s.at[i], e_r.at[i, c], diagonal))

    def y_copy(i):
        return pltpu.make_async_copy(y_stage(i), y_own.at[pl.ds(i * CHUNK, CHUNK)], io_s.at[i])

    loop(
        N_CHUNK,
        lambda i: second_norm(i, act, w, prm, mid, d_ffn, mine, y_stage(i), d_ffn, ngrad),
    )
    for i in range(2):
        y_copy(i).start()
    give_back(y_stage(2), y_back, 0, start)

    def spare(m, g):
        return gown.at[0, g] if m else act.at[2 + g, pl.ds(0, D)]

    def r_z(m, g, dz):
        return w.at[2, m, pl.ds(pl.multiple_of((g * nz + dz) * rows, rows), rows)]

    def core_send(m, g):
        return remote(spare(m, g), r_c.at[m, g], c_s.at[m, g], c_r.at[m, g], core)

    def fetch(m, g):
        return pltpu.make_async_copy(r_c.at[m, g], act.at[g, pl.ds(0, D)], stage_s.at[g])

    def core_fetch(m, g):
        arrived(r_c.at[m, g], c_r.at[m, g])
        fetch(m, g).start()

    def core_add(m, g):
        fetch(m, g).wait()

        def body(i):
            dz = i // 2 + 1
            zz = z_of(dz)
            xx = lax.rem(xc + 1 + i, 2)
            p = part(zz, xx)
            gown[m, g, p] = (gown[m, g, p].astype(F32) + act[g, p].astype(F32)).astype(BF)

        loop(2 * nz, body)
        for dz in range(1, nz + 1):
            zz = z_of(dz)
            remote(gown.at[m, g, part(zz, 1 - xc)], r_x.at[m, g, zz], x_s.at[m, g, zz], x_r.at[m, g, zz], other_x).start()

    def sum_event(q):
        m = 2 - q // (2 * nz)
        g = (q // nz) % 2
        dz = q % nz + 1
        zz = z_of(dz)
        arrived(r_x.at[m, g, zz], x_r.at[m, g, zz])
        p = part(zz, xc)
        gown[m, g, p] = (gown[m, g, p].astype(F32) + r_x[m, g, zz].astype(F32)).astype(BF)

        @pl.when(dz < nz)
        def _():
            remote(gown.at[m, g, p], r_z(m, g, dz), z_s.at[m, g, dz], z_r.at[m, g, dz], {"z": zz}).start()

    def own_copy(m):
        return pltpu.make_async_copy(mid.at[pl.ds(OWN_ROWS + m * rows, rows)], own_out.at[m], io_s.at[3 + m])

    def last_send(m):
        return remote(mid_low.at[pl.ds(EXT_ROWS + m * rows, rows)], oth_out.at[m], y_s.at[m], y_r.at[m], across)

    def finish(m, g):
        total = gown[m, g, part(z, xc)].astype(F32)
        for dz in range(1, nz):
            arrived(r_z(m, g, dz), z_r.at[m, g, dz])
            total += r_z(m, g, dz)[...].astype(F32)

        @pl.when(y == g)
        def _():
            mid[OWN_ROWS + m * rows : OWN_ROWS + (m + 1) * rows] = total
            own_copy(m).start()

        @pl.when(y != g)
        def _():
            mid_low[EXT_ROWS + m * rows : EXT_ROWS + (m + 1) * rows] = total.astype(BF)
            last_send(m).start()

    def slope_grads(m, a, b):
        def body(q):
            g = q % 2
            t = 2 * g + jnp.where(q < 2, 1 - c, c)
            dst = gown.at[jnp.where(q < 2, 0, m), g]
            for k in range(0, D, GW):
                dst[:, k : k + GW] = dot_tn(a[...], b[t, :, k : k + GW]).astype(BF)

            @pl.when(q < 2)
            def _():
                core_send(m, g).start()

        loop(4, body)

    slope_grads(2, d_ffn, act)

    def up_back(i):
        back_up(i // N_CHUNK, i % N_CHUNK, d_ffn, w, slope)

    def fetch_two(m):
        for g in range(2):
            core_fetch(m, g)

    def add_two(m):
        for g in range(2):
            core_add(m, g)

    def gather_over():
        loop(6, gather_sent)

    weave(
        GROUPS * N_CHUNK,
        up_back,
        {1: lambda: fetch_two(2), 3: lambda: add_two(2), 4: gather_over},
    )
    for dz in range(1, nz):
        pl.semaphore_signal(free_s, inc=1, device_id={"z": z_of(dz)}, device_id_type=MESH)
    for g in range(2):
        core_send(2, g).wait_send()
    for i in range(2):
        y_copy(i).wait()
    has_left(y_stage(2), e_s.at[0])
    slope_grads(1, mid_low, slope)
    fetch_two(1)
    pl.semaphore_wait(free_s, nz - 1)
    loop(2, sum_event)
    weave(
        N_CHUNK,
        lambda i: back_first_norm(i, slope, w, prm, mid, n1, s1, d_ffn, ngrad),
        {0: lambda: add_two(1), 1: lambda: sum_event(2)},
    )
    for g in range(2):
        core_send(1, g).wait_send()
    sum_event(3)

    def send_norms(i, act_on):
        if i == 0:
            act_on(remote(ngrad, n_c, ng_s.at[0], ng_r.at[0], core))
        elif i == 1:
            act_on(remote(n_c, n_x, ng_s.at[1], ng_r.at[1], other_x))
        elif i == 2:
            for dz in range(1, nz):
                act_on(remote(n_x, n_z.at[dz], ng_s.at[1 + dz], ng_r.at[1 + dz], {"z": z_of(dz)}))
        else:
            act_on(remote(n_out.at[y], n_out.at[y], ng_s.at[nz + 1], ng_r.at[nz + 1], across))

    send_norms(0, start)
    loop(GROUPS * N_CHUNK, lambda i: back_heads(i // N_CHUNK, i % N_CHUNK, d_ffn, wo, slope))
    sum_event(4)
    send_norms(0, recv)
    send_norms(0, lambda cp: cp.wait_send())
    n_c[...] += ngrad[...]
    send_norms(1, start)

    def attention_back(i):
        back_attend(i // per, [(i % per) * PAIR + k for k in range(PAIR)], proj, probs, slope)

        @pl.when(i % 2 == 1)
        def _():
            sum_event(5 + i // 2)

    loop(GROUPS * per, attention_back)
    send_norms(1, recv)
    send_norms(1, lambda cp: cp.wait_send())
    n_x[...] += n_c[...]
    send_norms(2, start)
    seen = 5 + GROUPS * per // 2

    def qkv_grads(q):
        g = q % 2

        def store(col, value):
            value = value.astype(BF)

            @pl.when(q < 2)
            def _():
                spare(0, g)[:, col : col + 128] = value

            @pl.when(q >= 2)
            def _():
                gown[0, g, :, col : col + 128] = value

        grad_qkv_out(2 * g + jnp.where(q < 2, 1 - c, c), x, proj, d_ffn, hout, store)

        @pl.when(q < 2)
        def _():
            core_send(0, g).start()

        sum_event(seen + q)

    loop(4, qkv_grads)
    seen += 4
    fetch_two(0)
    add_two(0)
    total = n_x[...]
    for dz in range(1, nz):
        arrived(n_z.at[dz], ng_r.at[1 + dz])
        total += n_z[dz]
    n_out[y] = total
    send_norms(3, start)

    def inputs_back(i):
        k = lax.rem(i + N_CHUNK - 1, N_CHUNK)

        def keep(r, grad):
            mid[r] = grad

            @pl.when(i == 0)
            def _():
                mid_low[:EXT_ROWS] = grad.astype(BF)

        back_input(k, proj, w, mid, keep)

        @pl.when(i == 0)
        def _():
            give_back(mid_low.at[pl.ds(0, EXT_ROWS)], g_back, 1, start)

        sum_event(seen + i)

    loop(N_CHUNK, inputs_back)
    seen += N_CHUNK
    g_copy = pltpu.make_async_copy(mid.at[pl.ds(0, OWN_ROWS)], g_own, io_s.at[2])
    g_copy.start()
    total_events = 6 * nz
    after = 4 * nz
    if seen < after:
        loop(after - seen, lambda q: sum_event(seen + q))
        seen = after
    for g in range(2):
        finish(2, g)
    loop(nz, lambda q: sum_event(after + q))
    for g in range(2):
        finish(1, g)
    loop(nz, lambda q: sum_event(after + nz + q))
    for g in range(2):
        finish(0, g)

    def sums_sent(i):
        m, g = i // 2, i % 2
        for dz in range(nz):
            if dz:
                has_left(r_x.at[0, 0, 0], z_s.at[m, g, dz])
            has_left(r_x.at[0, 0, 0], x_s.at[m, g, dz])

    loop(6, sums_sent)
    for g in range(2):
        core_send(0, g).wait_send()
    for m in range(3):
        has_left(mats[m].at[0], ys_s.at[m])
        own_copy(m).wait()
        last_send(m).wait()
    lend(x_in, x, 0, lambda cp: cp.wait_send())
    lend(cot, d_ffn, 1, lambda cp: cp.wait_send())
    for i in range(4):
        norm_hop(i, lambda cp: cp.wait_send())
    send_norms(2, lambda cp: cp.wait_send())
    send_norms(3, lambda cp: cp.wait())
    g_copy.wait()
    has_left(mid_low.at[pl.ds(0, EXT_ROWS)], e_s.at[1])

    @pl.when(lender)
    def _():
        for i, dst in enumerate((y_back, g_back)):
            for j in range(2):
                arrived(dst.at[pl.ds(j * EXT_ROWS, EXT_ROWS)], e_r.at[i, j])


def run_step(nz, tags, lens, x_in, cot, qo, up, dn, gain, bias):
    rows = up.shape[1]
    V = pl.BlockSpec(memory_space=pltpu.VMEM)
    S = pl.BlockSpec(memory_space=pltpu.SMEM)
    sem = pltpu.SemaphoreType.DMA
    out = jax.ShapeDtypeStruct
    return pl.pallas_call(
        partial(step_kernel, nz, rows),
        out_shape=(
            out((OWN_ROWS, D), BF),
            out((OWN_ROWS, D), F32),
            out((3, rows, D), F32),
            out((3, rows, D), BF),
            out((2, 8, D), F32),
            out((OWN_ROWS, D), BF),
            out((OWN_ROWS, D), BF),
            out((3, 2, D, D), BF),
        ),
        in_specs=[S, S, ANY, ANY, ANY, ANY, ANY, V, V],
        out_specs=(ANY, ANY, ANY, ANY, V, ANY, ANY, ANY),
        scratch_shapes=[
            pltpu.VMEM((3, GROUPS, D, D), BF),
            pltpu.VMEM((ROWS, D), BF),
            pltpu.VMEM((GROUPS, ROWS, D), BF),
            pltpu.VMEM((GROUPS, SLOTS, LENGTH, 512), BF),
            pltpu.VMEM((GROUPS, ROWS, GW), BF),
            pltpu.VMEM((GROUPS, D, GW), BF),
            pltpu.VMEM((ROWS, D), F32),
            pltpu.VMEM((ROWS, D), BF),
            pltpu.VMEM((ROWS, 128), F32),
            pltpu.VMEM((ROWS, D), BF),
            pltpu.VMEM((GROUPS, ROWS, D), BF),
            pltpu.VMEM((GROUPS, ROWS, D), BF),
            pltpu.VMEM((ROWS, D), BF),
            pltpu.VMEM((3, 2, D, D), BF),
            pltpu.VMEM((3, 2, nz, rows, D), BF),
            pltpu.VMEM((8 * nz, 8, 128), F32),
            pltpu.VMEM((8, D), F32),
            pltpu.VMEM((8, D), F32),
            pltpu.VMEM((8, D), F32),
            pltpu.VMEM((8, D), F32),
            pltpu.VMEM((nz, 8, D), F32),
            sem((5,)), sem((6,)), sem((2,)),
            sem((3,)), sem((3,)),
            sem((3, 2, 2, nz)), sem((3, 2, 2, nz)),
            sem((3, 2, nz)), sem((3, 2, nz)),
            sem((3, 2, nz, 2)), sem((3, 2, nz, 2)),
            sem((2, 2)), sem((2,)),
            sem((nz + 2,)), sem((nz + 2,)),
            sem((3, 2)), sem((3, 2)),
            sem((3, 2, nz)), sem((3, 2, nz)),
            sem((3, 2, nz)), sem((3, 2, nz)),
            sem((3,)), sem((3,)),
            sem((2,)), sem((2, 2)),
            sem((nz + 2,)), sem((nz + 2,)),
            pltpu.SemaphoreType.REGULAR,
        ],
        compiler_params=pltpu.CompilerParams(
            collective_id=0, has_side_effects=True, vmem_limit_bytes=67043328
        ),
        name="layer_step",
    )(tags, lens, x_in, cot, qo, up, dn, gain, bias)


def split_local(nz, x_in, tags, lengths, w_qkv, w_out, w_up, w_down, norm_gain, norm_bias, cotangent):
    z, x, y, c = place()
    rows = w_up.shape[1]
    cols = norm_gain.shape[2]
    qo = []
    for i in range(3):
        qo += [w_qkv[:, :, i], w_out[:, :, HEAD_DIM * i : HEAD_DIM * (i + 1)]]
    qo = jnp.concatenate(qo, -1)
    y_own, g_own, own_g, oth_g, n_sum, y_back, g_back, _ = run_step(
        nz, tags, lengths, x_in, cotangent, qo, w_up, w_down, norm_gain, norm_bias
    )
    kinds = lax.dynamic_slice_in_dim(tags, (2 * y + c) * OWN, OWN)
    mine = jnp.repeat(kinds == y, LENGTH)[:, None]
    y_out = jnp.where(mine, y_own, y_back)
    x_grad = jnp.where(mine, g_own, g_back.astype(F32))
    oth_g = oth_g.astype(F32)
    both = jnp.stack([jnp.where(y == 0, own_g, oth_g), jnp.where(y == 0, oth_g, own_g)])
    packed = both[:, 0].reshape(2, rows, 3, GW)
    me = ((z * 2 + x) * 2 + y) * 2 + c
    n_mine = lax.dynamic_slice_in_dim(n_sum, me * cols, cols, 2)
    return (
        y_out,
        x_grad,
        packed[..., : GW - HEAD_DIM],
        packed[..., GW - HEAD_DIM :].reshape(w_out.shape),
        both[:, 1],
        both[:, 2],
        n_mine[:, :2],
        n_mine[:, 2:4],
    )


def typed_map(operand, stacked, chain_kinds, pattern):

    def single(element):
        weight = lax.dynamic_index_in_dim(stacked, element[1], 0, keepdims=False)
        return jnp.einsum(pattern, element[0], weight, preferred_element_type=jnp.float32)

    return lax.map(single, (operand, chain_kinds))


def typed_grads(running, operand, partner, chain_kinds, pattern):

    def single(carry, element):
        product_term = jnp.einsum(
            pattern, element[0], element[1], preferred_element_type=jnp.float32
        )
        previous = lax.dynamic_index_in_dim(carry, element[2], 0, keepdims=False)
        return (
            lax.dynamic_update_index_in_dim(carry, previous + product_term, element[2], 0),
            None,
        )

    return lax.scan(single, running, (operand, partner, chain_kinds))[0]


def row_terms(operand, stacked, chain_kinds, pattern, row_count):
    result = typed_map(operand, stacked, chain_kinds, pattern)
    return result.reshape(row_count, result.shape[-1])


def old_norm_forward(values, gain_rows, shift_rows):
    center = values - jnp.mean(values, -1, keepdims=True)
    factor = lax.rsqrt(jnp.mean(center * center, -1, keepdims=True) + EPS)
    normed = center * factor
    return (normed * gain_rows + shift_rows, normed, factor)


def old_norm_backward(grad_out, normed, factor, gain_rows):
    scaled = grad_out * gain_rows
    mean_plain = jnp.mean(scaled, -1, keepdims=True)
    mean_normed = jnp.mean(scaled * normed, -1, keepdims=True)
    return factor * (scaled - mean_plain - normed * mean_normed)


def type_sums(onehot, values):
    return jnp.dot(onehot.T, values, precision=HIGH, preferred_element_type=jnp.float32)


def general_local(x_in, tags, lengths, w_qkv, w_out, w_up, w_down, norm_gain, norm_bias, cotangent):
    tp_count = lax.axis_size("tensor")
    tp_index = lax.axis_index("tensor")
    local_rows = CHAINS_PART * LENGTH
    batch_chains = tp_count * CHAINS_PART
    head_cols = w_qkv.shape[3]
    local_heads = head_cols // HEAD_DIM
    tag_grid = tags.reshape(tp_count, MICRO, CHAINS_PART)
    len_grid = lengths.reshape(tp_count, MICRO, CHAINS_PART)
    own_tags = lax.dynamic_index_in_dim(tag_grid, tp_index, 0, keepdims=False)
    gains, shifts = (
        lax.all_gather(norm_gain, ("dp", "tensor"), axis=2, tiled=True),
        lax.all_gather(norm_bias, ("dp", "tensor"), axis=2, tiled=True),
    )
    grad_full = (
        jnp.zeros((2, D, 3, head_cols), jnp.float32),
        jnp.zeros((2, D, head_cols), jnp.float32),
        jnp.zeros((2, D, w_up.shape[2]), jnp.float32),
        jnp.zeros((2, D, w_down.shape[2]), jnp.float32),
    )
    shards = (
        jnp.zeros(w_qkv.shape, jnp.float32),
        jnp.zeros(w_out.shape, jnp.float32),
        jnp.zeros(w_up.shape, jnp.float32),
        jnp.zeros(w_down.shape, jnp.float32),
    )
    gain_acc = jnp.zeros((2, 2, D), jnp.float32)
    shift_acc = jnp.zeros((2, 2, D), jnp.float32)
    outputs = []
    input_grads = []
    for micro_index in range(MICRO):
        held = (
            lax.all_gather(w_qkv, "dp", axis=1, tiled=True),
            lax.all_gather(w_out, "dp", axis=1, tiled=True),
            lax.all_gather(w_up, "dp", axis=1, tiled=True),
            lax.all_gather(w_down, "dp", axis=1, tiled=True),
        )
        qkv_w, out_w, up_w, down_w = held
        chain_kinds = tag_grid[:, micro_index].reshape(batch_chains)
        chain_lens = len_grid[:, micro_index].reshape(batch_chains)
        own_rows = x_in[micro_index * local_rows : (micro_index + 1) * local_rows]
        kinds_rows = jnp.repeat(own_tags[micro_index], LENGTH)
        heavy_rows = (kinds_rows == 0)[:, None]
        onehot = (kinds_rows[:, None] == jnp.arange(2)[None, :]).astype(jnp.float32)
        gain_mid = jnp.where(heavy_rows, gains[0, 0], gains[1, 0])
        shift_mid = jnp.where(heavy_rows, shifts[0, 0], shifts[1, 0])
        gain_end = jnp.where(heavy_rows, gains[0, 1], gains[1, 1])
        shift_end = jnp.where(heavy_rows, shifts[0, 1], shifts[1, 1])
        gathered = lax.all_gather(own_rows, "tensor", axis=0, tiled=True).reshape(
            batch_chains, LENGTH, D
        )
        projected = typed_map(gathered, qkv_w, chain_kinds, "ld,dkh->lkh").astype(jnp.bfloat16)
        query = projected[:, :, 0].reshape(batch_chains, LENGTH, local_heads, HEAD_DIM)
        keys_low = projected[:, :, 1].reshape(batch_chains, LENGTH, local_heads, HEAD_DIM)
        values_low = projected[:, :, 2].reshape(batch_chains, LENGTH, local_heads, HEAD_DIM)
        valid = (
            lax.broadcasted_iota(jnp.int32, (batch_chains, 1, 1, LENGTH), 3)
            < chain_lens[:, None, None, None]
        )
        scores = (
            jnp.einsum("cqhe,ckhe->chqk", query, keys_low, preferred_element_type=jnp.float32)
            * 0.125
        )
        scores = jnp.where(valid, scores, NEG)
        highest = jnp.max(scores, -1, keepdims=True)
        expo = jnp.exp(scores - highest)
        totals = jnp.sum(expo, -1, keepdims=True)
        probs = expo / totals
        log_total = highest + jnp.log(totals)
        heads_low = jnp.einsum(
            "chqk,ckhe->cqhe",
            probs.astype(jnp.bfloat16),
            values_low,
            preferred_element_type=jnp.float32,
        ).astype(jnp.bfloat16)
        heads_low = heads_low.reshape(batch_chains, LENGTH, head_cols)
        attn_sum = lax.psum_scatter(
            row_terms(
                heads_low, out_w, chain_kinds, "lh,dh->ld", lax.axis_size("tensor") * local_rows
            ).astype(jnp.bfloat16),
            "tensor",
            scatter_dimension=0,
            tiled=True,
        ).astype(jnp.float32)
        mid, normed_mid, factor_mid = old_norm_forward(
            own_rows.astype(jnp.float32) + attn_sum, gain_mid, shift_mid
        )
        mid_all = lax.all_gather(mid.astype(jnp.bfloat16), "tensor", axis=0, tiled=True).reshape(
            batch_chains, LENGTH, D
        )
        up_value = typed_map(mid_all, up_w, chain_kinds, "ld,df->lf")
        act_low = jax.nn.gelu(up_value, approximate=False).astype(jnp.bfloat16)
        ffn_sum = lax.psum_scatter(
            row_terms(
                act_low, down_w, chain_kinds, "lf,df->ld", lax.axis_size("tensor") * local_rows
            ).astype(jnp.bfloat16),
            "tensor",
            scatter_dimension=0,
            tiled=True,
        ).astype(jnp.float32)
        final, normed_end, factor_end = old_norm_forward(ffn_sum + mid, gain_end, shift_end)
        outputs.append(final.astype(jnp.bfloat16))
        base = grad_full
        grad_final = cotangent[micro_index * local_rows : (micro_index + 1) * local_rows].astype(
            jnp.float32
        )
        gain_acc = gain_acc.at[:, 1].add(type_sums(onehot, grad_final * normed_end))
        shift_acc = shift_acc.at[:, 1].add(type_sums(onehot, grad_final))
        grad_resid2 = old_norm_backward(grad_final, normed_end, factor_end, gain_end)
        grad_ffn = lax.all_gather(
            grad_resid2.astype(jnp.bfloat16), "tensor", axis=0, tiled=True
        ).reshape(batch_chains, LENGTH, D)
        grad_act = typed_map(grad_ffn, down_w, chain_kinds, "ld,df->lf")
        unused_value, gelu_back = jax.vjp(partial(jax.nn.gelu, approximate=False), up_value)
        grad_up = gelu_back(grad_act)[0].astype(jnp.bfloat16)
        down_acc = typed_grads(base[3], grad_ffn, act_low, chain_kinds, "ld,lf->df")
        up_acc = typed_grads(base[2], mid_all, grad_up, chain_kinds, "ld,lf->df")
        grad_mid = grad_resid2 + lax.psum_scatter(
            row_terms(
                grad_up, up_w, chain_kinds, "lf,df->ld", lax.axis_size("tensor") * local_rows
            ).astype(jnp.bfloat16),
            "tensor",
            scatter_dimension=0,
            tiled=True,
        ).astype(jnp.float32)
        gain_acc = gain_acc.at[:, 0].add(type_sums(onehot, grad_mid * normed_mid))
        shift_acc = shift_acc.at[:, 0].add(type_sums(onehot, grad_mid))
        grad_resid1 = old_norm_backward(grad_mid, normed_mid, factor_mid, gain_mid)
        grad_attn = lax.all_gather(
            grad_resid1.astype(jnp.bfloat16), "tensor", axis=0, tiled=True
        ).reshape(batch_chains, LENGTH, D)
        grad_heads = typed_map(grad_attn, out_w, chain_kinds, "ld,dh->lh").astype(jnp.bfloat16)
        out_acc = typed_grads(base[1], grad_attn, heads_low, chain_kinds, "ld,lh->dh")
        grad_heads = grad_heads.reshape(batch_chains, LENGTH, local_heads, HEAD_DIM)
        again = (
            jnp.einsum("cqhe,ckhe->chqk", query, keys_low, preferred_element_type=jnp.float32)
            * 0.125
        )
        probs_again = jnp.exp(jnp.where(valid, again, NEG) - log_total)
        grad_probs = jnp.einsum(
            "cqhe,ckhe->chqk", grad_heads, values_low, preferred_element_type=jnp.float32
        )
        inner = jnp.sum(grad_probs * probs_again, -1, keepdims=True)
        grad_scores = (probs_again * (grad_probs - inner)).astype(jnp.bfloat16)
        grad_query = (
            jnp.einsum("chqk,ckhe->cqhe", grad_scores, keys_low, preferred_element_type=jnp.float32)
            * 0.125
        ).astype(jnp.bfloat16)
        grad_keys = (
            jnp.einsum("chqk,cqhe->ckhe", grad_scores, query, preferred_element_type=jnp.float32)
            * 0.125
        ).astype(jnp.bfloat16)
        grad_values = jnp.einsum(
            "chqk,cqhe->ckhe",
            probs_again.astype(jnp.bfloat16),
            grad_heads,
            preferred_element_type=jnp.float32,
        ).astype(jnp.bfloat16)
        grad_proj = jnp.stack([grad_query, grad_keys, grad_values], 2).reshape(
            batch_chains, LENGTH, 3, head_cols
        )
        qkv_acc = typed_grads(base[0], gathered, grad_proj, chain_kinds, "ld,lkh->dkh")
        grad_input = grad_resid1 + lax.psum_scatter(
            row_terms(
                grad_proj, qkv_w, chain_kinds, "lkh,dkh->ld", lax.axis_size("tensor") * local_rows
            ).astype(jnp.bfloat16),
            "tensor",
            scatter_dimension=0,
            tiled=True,
        ).astype(jnp.float32)
        input_grads.append(grad_input)
        updated = (qkv_acc, out_acc, up_acc, down_acc)
        grad_full = updated
    shards = (
        lax.psum_scatter(grad_full[0], "dp", scatter_dimension=1, tiled=True),
        lax.psum_scatter(grad_full[1], "dp", scatter_dimension=1, tiled=True),
        lax.psum_scatter(grad_full[2], "dp", scatter_dimension=1, tiled=True),
        lax.psum_scatter(grad_full[3], "dp", scatter_dimension=1, tiled=True),
    )
    gain_grad, shift_grad = (
        lax.psum_scatter(gain_acc, ("dp", "tensor"), scatter_dimension=2, tiled=True),
        lax.psum_scatter(shift_acc, ("dp", "tensor"), scatter_dimension=2, tiled=True),
    )
    return (
        jnp.concatenate(outputs, 0),
        jnp.concatenate(input_grads, 0),
        shards[0],
        shards[1],
        shards[2],
        shards[3],
        gain_grad,
        shift_grad,
    )


def solution(mesh):
    placed = (
        P(("dp", "tensor"), None),
        P("dp"),
        P("dp"),
        P(None, "dp", None, "tensor"),
        P(None, "dp", "tensor"),
        P(None, "dp", "tensor"),
        P(None, "dp", "tensor"),
        P(None, None, ("dp", "tensor")),
        P(None, None, ("dp", "tensor")),
        P(("dp", "tensor"), None),
    )
    results = (
        P(("dp", "tensor"), None),
        P(("dp", "tensor"), None),
        P(None, "dp", None, "tensor"),
        P(None, "dp", "tensor"),
        P(None, "dp", "tensor"),
        P(None, "dp", "tensor"),
        P(None, None, ("dp", "tensor")),
        P(None, None, ("dp", "tensor")),
    )
    n_dp, n_tensor = mesh.shape["dp"], mesh.shape["tensor"]
    if n_tensor != GROUPS or n_dp not in (8, 16):
        return jax.shard_map(
            general_local, mesh=mesh, in_specs=placed, out_specs=results, check_vma=False
        )
    fine = Mesh(mesh.devices.reshape(n_dp // 2, 2, 2, 2), AXES)
    names = {"dp": ("z", "x"), "tensor": ("y", "c")}

    def refine(spec):
        parts = []
        for entry in spec:
            entry = (entry,) if isinstance(entry, str) else entry
            parts.append(entry and sum((names[a] for a in entry), ()))
        return P(*parts)

    return jax.shard_map(
        partial(split_local, n_dp // 2),
        mesh=fine,
        in_specs=tuple(refine(s) for s in placed),
        out_specs=tuple(refine(s) for s in results),
        check_vma=False,
    )
```

profile of v0, /device:TPU:5, one launch (start us, length us, event | category | flops | bytes accessed | tf_op | source)
XLA Modules:
  0.0 230.8 jit_solution(12274102842485028365)
XLA Ops:
  0.6 1.0 slice_bitcast_fusion
  1.7 1.0 fusion.6
  2.6 0.9 concatenate.3.qo
  3.5 216.6 %layer_step.1 = (bf16[640,768]{1,0:T(8,128)(2,1)}, f32[640,768]{1,0:T(8,128)}, f32[3,96,768]{2,1,0:T(8,128)}, bf16[3,96,768]{2,1,0:T(8,128)(2,1)}, f32[2,8,768]{...) custom-call(s32[16]{0:T(128)} %tags.1, s32[16]{0:T(128)} %lens.1, ...), custom_call_target="tpu_custom_call" | custom-call | tf_op jit(solution)/shard_map/layer_step/pallas_call | solution.py:825
  220.1 1.4 fusion.1
  221.5 1.1 fusion.5
  222.7 0.0 copy-start.3
  222.7 0.0 copy-start
  222.7 0.3 reshape_squeeze.3
  223.0 0.3 slice.55
  223.2 0.1 copy.25
  223.4 0.8 copy.27
  224.2 0.9 copy.26
  225.1 0.0 copy-done.3
  225.1 0.1 dynamic-slice_compare_fusion
  225.2 0.1 broadcast_in_dim.19
  225.3 0.1 broadcast_in_dim.20
  225.4 0.0 copy-done
  225.4 0.0 copy-start.2
  225.4 2.9 %convert_select_fusion = f32[640,768]{1,0:T(8,128)} fusion(f32[640,768]{1,0:T(8,128)S(1)} %copy-done, bf16[640,768]{1,0:T(8,128)(2,1)} %get-tuple-element.18, pred[640]{0:T(1024)(128)(4,1)S(1)} %broadcast_in_dim.20), kind=kLoop, calls=%fused_computation.4 | loop fusion | flops 983040 | bytes 4915840 | tf_op jit(solution)/shard_map/jit(_where)/select_n | solution.py:897
  228.3 0.0 copy-done.1
  228.3 0.0 copy-done.2
  228.3 1.1 broadcast_select_fusion
  229.4 1.4 constant_dynamic-slice_fusion.1
  (1 shorter events, 0.0 us)
Async XLA Ops:
  222.7 2.5 %copy-start.3 = (s32[16]{0:T(128)S(1)}, s32[16]{0:T(128)}, u32[]{:S(2)}) copy-start(s32[16]{0:T(128)} %tags.1) | copy-start | bytes 196
  222.7 2.7 %copy-start = (f32[640,768]{1,0:T(8,128)S(1)}, f32[640,768]{1,0:T(8,128)}, u32[]{:S(2)}) copy-start(f32[640,768]{1,0:T(8,128)} %get-tuple-element.17) | copy-start | bytes 5898244
  225.4 2.9 %copy-start.1 = (bf16[640,768]{1,0:T(8,128)(2,1)S(1)}, bf16[640,768]{1,0:T(8,128)(2,1)}, u32[]{:S(2)}) copy-start(bf16[640,768]{1,0:T(8,128)(2,1)} %get-tuple-element.15) | copy-start | bytes 2949124
  225.4 2.9 %copy-start.2 = (bf16[640,768]{1,0:T(8,128)(2,1)S(1)}, bf16[640,768]{1,0:T(8,128)(2,1)}, u32[]{:S(2)}) copy-start(bf16[640,768]{1,0:T(8,128)(2,1)} %get-tuple-element.16) | copy-start | bytes 2949124
where the time goes:
time: 235 us; the launch traced here: 231 us
  Pallas kernels  217 us (92%)
  local copies, waits for them, and re-layouts  6.92 us (3%)
  other arithmetic  6.6 us (3%)
    pallas_call x1, Pallas kernels, run_step(): pl.pallas_call(partial(step_kernel, nz, rows), out_shape=(out((OWN_ROWS,...  217 us

commit v1 on v0

--- a/solution.py
+++ b/solution.py
@@ -179,12 +179,13 @@
         slope[t, r, k : k + GW] = (cdf + up * bell).astype(BF)
 
 
-def second_norm(i, act, w, prm, mid, cot, mine, y_rows, d_ffn, ngrad):
+def feed_down(i, t, act, w, mid):
     r = chunk_rows(i)
-    ffn = dot_nt(act[0, r], w[2, 0])
-    for t in range(1, GROUPS):
-        ffn += dot_nt(act[t, r], w[2, t])
-    mid[r] += ffn
+    mid[r] += dot_nt(act[t, r], w[2, t]) + dot_nt(act[t + 1, r], w[2, t + 1])
+
+
+def second_norm(i, t, act, w, prm, mid, cot, mine, y_rows, d_ffn, ngrad):
+    feed_down(i, t, act, w, mid)
 
     def piece(p, k):
         normed, factor = norm_rows(mid[p])
@@ -284,11 +285,11 @@
 def step_kernel(nz, rows,
                 tags, lens, x_in, cot, qo, up, dn, gain, bias,
                 y_own, g_own, own_out, oth_out, n_out, y_back, g_back, r_c,
-                w, x, proj, probs, hout, wo, mid, n1, s1, mid_low, act, slope, d_ffn, gown, r_x,
+                w, x, proj, probs, hout, wo, mid, n1, s1, mid_low, act, slope, d_ffn, gown, r_x, r_z,
                 n_all, prm, ngrad, n_c, n_x, n_z,
                 load_s, io_s, stage_s,
                 ys_s, ys_r, zs_s, zs_r, xs_s, xs_r, cs_s, cs_r, ex_s, ex_r, na_s, na_r,
-                c_s, c_r, x_s, x_r, z_s, z_r, y_s, y_r, e_s, e_r, ng_s, ng_r, free_s):
+                c_s, c_r, x_s, x_r, z_s, z_r, y_s, y_r, e_s, e_r, ng_s, ng_r):
     z, xc, y, c = place()
     core, across, other_x = {"c": 1 - c}, {"y": 1 - y}, {"x": 1 - xc}
     diagonal = {"y": 1 - y, "c": 1 - c}
@@ -381,16 +382,13 @@
 
         loop(2, body)
 
-    def own_xc(m):
-        def body(g):
-            x_copy(m, g, z).start()
-            c_copy(m, g, z, xc).start()
-
-        loop(2, body)
-
-    def z_event(m, j):
+    def own_xc(m, g):
+        x_copy(m, g, z).start()
+        c_copy(m, g, z, xc).start()
+
+    def z_event(m, j, first=0, last=2):
         def body(q):
-            g, d = q // 2, q % 2
+            g, d = first + q // 2, q % 2
             zz = z - j + 2 * j * d
 
             @pl.when(inside(zz))
@@ -401,11 +399,11 @@
                 x_copy(m, g, zz).start()
                 c_copy(m, g, zz, xc).start()
 
-        loop(4, body)
-
-    def x_event(m, j):
+        loop(2 * (last - first), body)
+
+    def x_event(m, j, first=0, last=2):
         def body(q):
-            g, d = q // 2, q % 2
+            g, d = first + q // 2, q % 2
             zz = z - j + 2 * j * d
 
             @pl.when(jnp.logical_and(inside(zz), j + 1 > d))
@@ -413,15 +411,16 @@
                 arrived(block(m, g, zz, 1 - xc), xs_r.at[m, g, zz])
                 c_copy(m, g, zz, 1 - xc).start()
 
-        loop(4, body)
-
-    def gathered(m):
+        loop(2 * (last - first), body)
+
+    def gathered(m, first=0, last=2):
         def body(i):
-            t = 2 * lax.rem(y + i // (2 * nz), 2) + 1 - c
+            g = first + i // (2 * nz)
+            t = 2 * lax.rem(y + g, 2) + 1 - c
             zz, xx = (i // 2) % nz, i % 2
-            arrived(w.at[m, t, part(zz, xx)], cs_r.at[m, i // (2 * nz), zz, xx])
-
-        loop(4 * nz, body)
+            arrived(w.at[m, t, part(zz, xx)], cs_r.at[m, g, zz, xx])
+
+        loop(2 * nz * (last - first), body)
 
     def gather_sent(i):
         m, g = i // 2, i % 2
@@ -454,7 +453,8 @@
         loads[m].wait()
     norm_hop(0, start)
     own_z(0)
-    own_xc(0)
+    for g in range(2):
+        own_xc(0, g)
     z_event(0, 1)
     norm_hop(0, recv)
     norm_hop(1, start)
@@ -466,7 +466,8 @@
         own_z(1)
     norm_hop(1, recv)
     norm_hop(2, start)
-    own_xc(1)
+    for g in range(2):
+        own_xc(1, g)
     x_event(0, 0)
     x_event(0, 1)
     for j in range(1, nz - 1):
@@ -490,12 +491,22 @@
 
     def more_own():
         z_event(1, nz - 1)
-        own_xc(2)
+        own_xc(2, 0)
 
     weave(
         GROUPS * N_CHUNK,
         projection,
-        {0: more_own, 8: lambda: x_event(1, 0), 11: lambda: z_event(2, 1)},
+        {0: more_own, 8: lambda: x_event(1, 0), 11: lambda: z_event(2, 1, 0, 1)},
+    )
+    per = SLOTS // PAIR
+
+    def attention(i):
+        attend(i // per, [(i % per) * PAIR + k for k in range(PAIR)], length_of, proj, probs, hout)
+
+    weave(
+        GROUPS * per,
+        attention,
+        {2: lambda: x_event(1, 1), 3: lambda: z_event(2, 2, 0, 1), 7: lambda: x_event(1, 2)},
     )
     norm_hop(3, recv)
     lane = lanes((2, D))
@@ -512,29 +523,37 @@
                 shifts += piece
     prm[0:2] = gains
     prm[2:4] = shifts
-    per = SLOTS // PAIR
-
-    def attention(i):
-        attend(i // per, [(i % per) * PAIR + k for k in range(PAIR)], length_of, proj, probs, hout)
-
-    weave(
-        GROUPS * per,
-        attention,
-        {2: lambda: x_event(1, 1), 3: lambda: z_event(2, 2), 7: lambda: x_event(1, 2)},
-    )
     loop(N_CHUNK, lambda i: first_norm(i, x, hout, wo, prm, mid, n1, s1, mid_low))
     for j in range(3, nz):
-        z_event(2, j)
+        z_event(2, j, 0, 1)
         x_event(1, j)
+    own_xc(2, 1)
     gathered(1)
     weave(
         GROUPS * N_CHUNK,
         lambda i: feed_up(i // N_CHUNK, i % N_CHUNK, mid_low, w, act, slope),
-        {2: lambda: x_event(2, 0), 7: lambda: x_event(2, 1)},
+        {
+            0: lambda: z_event(2, 1, 1, 2),
+            2: lambda: x_event(2, 0, 0, 1),
+            4: lambda: z_event(2, 2, 1, 2),
+            7: lambda: x_event(2, 1, 0, 1),
+        },
     )
     for j in range(2, nz):
-        x_event(2, j)
-    gathered(2)
+        if j > 2:
+            z_event(2, j, 1, 2)
+        x_event(2, j, 0, 1)
+    gathered(2, 0, 1)
+    first_two = 2 * y
+    last_two = 2 - first_two
+    weave(
+        N_CHUNK,
+        lambda i: feed_down(i, first_two, act, w, mid),
+        {0: lambda: x_event(2, 0, 1, 2), 2: lambda: x_event(2, 1, 1, 2)},
+    )
+    for j in range(2, nz):
+        x_event(2, j, 1, 2)
+    gathered(2, 1, 2)
     loads[4].wait()
     arrived(d_ffn.at[pl.ds(OWN_ROWS, EXT_ROWS)], ex_r.at[1])
 
@@ -557,23 +576,22 @@
 
     loop(
         N_CHUNK,
-        lambda i: second_norm(i, act, w, prm, mid, d_ffn, mine, y_stage(i), d_ffn, ngrad),
+        lambda i: second_norm(
+            i, last_two, act, w, prm, mid, d_ffn, mine, y_stage(i), d_ffn, ngrad
+        ),
     )
     for i in range(2):
         y_copy(i).start()
     give_back(y_stage(2), y_back, 0, start)
 
     def spare(m, g):
-        return gown.at[0, g] if m else act.at[2 + g, pl.ds(0, D)]
-
-    def r_z(m, g, dz):
-        return w.at[2, m, pl.ds(pl.multiple_of((g * nz + dz) * rows, rows), rows)]
+        return gown.at[0, g] if m else act.at[2 * g + c, pl.ds(0, D)]
 
     def core_send(m, g):
         return remote(spare(m, g), r_c.at[m, g], c_s.at[m, g], c_r.at[m, g], core)
 
     def fetch(m, g):
-        return pltpu.make_async_copy(r_c.at[m, g], act.at[g, pl.ds(0, D)], stage_s.at[g])
+        return pltpu.make_async_copy(r_c.at[m, g], act.at[2 * g + 1 - c, pl.ds(0, D)], stage_s.at[g])
 
     def core_fetch(m, g):
         arrived(r_c.at[m, g], c_r.at[m, g])
@@ -587,7 +605,7 @@
             zz = z_of(dz)
             xx = lax.rem(xc + 1 + i, 2)
             p = part(zz, xx)
-            gown[m, g, p] = (gown[m, g, p].astype(F32) + act[g, p].astype(F32)).astype(BF)
+            gown[m, g, p] = (gown[m, g, p].astype(F32) + act[2 * g + 1 - c, p].astype(F32)).astype(BF)
 
         loop(2 * nz, body)
         for dz in range(1, nz + 1):
@@ -605,7 +623,7 @@
 
         @pl.when(dz < nz)
         def _():
-            remote(gown.at[m, g, p], r_z(m, g, dz), z_s.at[m, g, dz], z_r.at[m, g, dz], {"z": zz}).start()
+            remote(gown.at[m, g, p], r_z.at[m, g, dz], z_s.at[m, g, dz], z_r.at[m, g, dz], {"z": zz}).start()
 
     def own_copy(m):
         return pltpu.make_async_copy(mid.at[pl.ds(OWN_ROWS + m * rows, rows)], own_out.at[m], io_s.at[3 + m])
@@ -616,8 +634,8 @@
     def finish(m, g):
         total = gown[m, g, part(z, xc)].astype(F32)
         for dz in range(1, nz):
-            arrived(r_z(m, g, dz), z_r.at[m, g, dz])
-            total += r_z(m, g, dz)[...].astype(F32)
+            arrived(r_z.at[m, g, dz], z_r.at[m, g, dz])
+            total += r_z[m, g, dz].astype(F32)
 
         @pl.when(y == g)
         def _():
@@ -629,8 +647,8 @@
             mid_low[EXT_ROWS + m * rows : EXT_ROWS + (m + 1) * rows] = total.astype(BF)
             last_send(m).start()
 
-    def slope_grads(m, a, b):
-        def body(q):
+    def slope_grads(m, a, b, extra):
+        def unit(q):
             g = q % 2
             t = 2 * g + jnp.where(q < 2, 1 - c, c)
             dst = gown.at[jnp.where(q < 2, 0, m), g]
@@ -641,48 +659,49 @@
             def _():
                 core_send(m, g).start()
 
-        loop(4, body)
-
-    slope_grads(2, d_ffn, act)
+        weave(4, unit, extra)
+
+    def then(*steps):
+        def run():
+            for f, *args in steps:
+                f(*args)
+
+        return run
+
+    def core_over(m):
+        for g in range(2):
+            core_send(m, g).wait_send()
+
+    slope_grads(
+        2,
+        d_ffn,
+        act,
+        {
+            1: then((core_fetch, 2, 0)),
+            2: then((core_fetch, 2, 1), (core_add, 2, 0)),
+            3: then((core_add, 2, 1), (core_over, 2)),
+        },
+    )
 
     def up_back(i):
         back_up(i // N_CHUNK, i % N_CHUNK, d_ffn, w, slope)
 
-    def fetch_two(m):
-        for g in range(2):
-            core_fetch(m, g)
-
-    def add_two(m):
-        for g in range(2):
-            core_add(m, g)
-
-    def gather_over():
-        loop(6, gather_sent)
-
-    weave(
-        GROUPS * N_CHUNK,
-        up_back,
-        {1: lambda: fetch_two(2), 3: lambda: add_two(2), 4: gather_over},
-    )
-    for dz in range(1, nz):
-        pl.semaphore_signal(free_s, inc=1, device_id={"z": z_of(dz)}, device_id_type=MESH)
-    for g in range(2):
-        core_send(2, g).wait_send()
+    weave(GROUPS * N_CHUNK, up_back, {7: then((sum_event, 0)), 11: then((sum_event, 1))})
     for i in range(2):
         y_copy(i).wait()
     has_left(y_stage(2), e_s.at[0])
-    slope_grads(1, mid_low, slope)
-    fetch_two(1)
-    pl.semaphore_wait(free_s, nz - 1)
-    loop(2, sum_event)
+    slope_grads(1, mid_low, slope, {1: then((sum_event, 2)), 3: then((sum_event, 3))})
+    for g in range(2):
+        core_fetch(1, g)
     weave(
         N_CHUNK,
         lambda i: back_first_norm(i, slope, w, prm, mid, n1, s1, d_ffn, ngrad),
-        {0: lambda: add_two(1), 1: lambda: sum_event(2)},
-    )
-    for g in range(2):
-        core_send(1, g).wait_send()
-    sum_event(3)
+        {
+            0: then((core_add, 1, 0), (core_add, 1, 1), (core_over, 1)),
+            1: then((sum_event, 4)),
+            2: then((sum_event, 5)),
+        },
+    )
 
     def send_norms(i, act_on):
         if i == 0:
@@ -697,7 +716,7 @@
 
     send_norms(0, start)
     loop(GROUPS * N_CHUNK, lambda i: back_heads(i // N_CHUNK, i % N_CHUNK, d_ffn, wo, slope))
-    sum_event(4)
+    sum_event(6)
     send_norms(0, recv)
     send_norms(0, lambda cp: cp.wait_send())
     n_c[...] += ngrad[...]
@@ -708,14 +727,10 @@
 
         @pl.when(i % 2 == 1)
         def _():
-            sum_event(5 + i // 2)
+            sum_event(7 + i // 2)
 
     loop(GROUPS * per, attention_back)
-    send_norms(1, recv)
-    send_norms(1, lambda cp: cp.wait_send())
-    n_x[...] += n_c[...]
-    send_norms(2, start)
-    seen = 5 + GROUPS * per // 2
+    seen = 7 + GROUPS * per // 2
 
     def qkv_grads(q):
         g = q % 2
@@ -737,19 +752,16 @@
         def _():
             core_send(0, g).start()
 
-        sum_event(seen + q)
-
-    loop(4, qkv_grads)
-    seen += 4
-    fetch_two(0)
-    add_two(0)
-    total = n_x[...]
-    for dz in range(1, nz):
-        arrived(n_z.at[dz], ng_r.at[1 + dz])
-        total += n_z[dz]
-    n_out[y] = total
-    send_norms(3, start)
-
+    weave(
+        4,
+        qkv_grads,
+        {
+            1: then((sum_event, seen)),
+            2: then((core_fetch, 0, 0), (core_fetch, 0, 1), (sum_event, seen + 1)),
+            3: then((core_add, 0, 0), (core_add, 0, 1), (sum_event, seen + 2)),
+        },
+    )
+    seen += 3
     def inputs_back(i):
         k = lax.rem(i + N_CHUNK - 1, N_CHUNK)
 
@@ -766,10 +778,8 @@
         def _():
             give_back(mid_low.at[pl.ds(0, EXT_ROWS)], g_back, 1, start)
 
-        sum_event(seen + i)
-
-    loop(N_CHUNK, inputs_back)
-    seen += N_CHUNK
+    weave(N_CHUNK, inputs_back, {1: then((sum_event, seen)), 2: then((sum_event, seen + 1))})
+    seen += 2
     g_copy = pltpu.make_async_copy(mid.at[pl.ds(0, OWN_ROWS)], g_own, io_s.at[2])
     g_copy.start()
     total_events = 6 * nz
@@ -780,9 +790,19 @@
     for g in range(2):
         finish(2, g)
     loop(nz, lambda q: sum_event(after + q))
+    send_norms(1, recv)
+    send_norms(1, lambda cp: cp.wait_send())
+    n_x[...] += n_c[...]
+    send_norms(2, start)
     for g in range(2):
         finish(1, g)
     loop(nz, lambda q: sum_event(after + nz + q))
+    total = n_x[...]
+    for dz in range(1, nz):
+        arrived(n_z.at[dz], ng_r.at[1 + dz])
+        total += n_z[dz]
+    n_out[y] = total
+    send_norms(3, start)
     for g in range(2):
         finish(0, g)
 
@@ -794,6 +814,7 @@
             has_left(r_x.at[0, 0, 0], x_s.at[m, g, dz])
 
     loop(6, sums_sent)
+    loop(6, gather_sent)
     for g in range(2):
         core_send(0, g).wait_send()
     for m in range(3):
@@ -852,6 +873,7 @@
             pltpu.VMEM((ROWS, D), BF),
             pltpu.VMEM((3, 2, D, D), BF),
             pltpu.VMEM((3, 2, nz, rows, D), BF),
+            pltpu.VMEM((3, 2, nz, rows, D), BF),
             pltpu.VMEM((8 * nz, 8, 128), F32),
             pltpu.VMEM((8, D), F32),
             pltpu.VMEM((8, D), F32),
@@ -871,7 +893,6 @@
             sem((3,)), sem((3,)),
             sem((2,)), sem((2, 2)),
             sem((nz + 2,)), sem((nz + 2,)),
-            pltpu.SemaphoreType.REGULAR,
         ],
         compiler_params=pltpu.CompilerParams(
             collective_id=0, has_side_effects=True, vmem_limit_bytes=67043328

time: 235 us -> 218 us (0.928)
  Pallas kernels: 217 us -> 201 us
    pallas_call x1, Pallas kernels: 217 us -> 201 us  [run_step(): pl.pallas_call(partial(step_kernel, nz, rows), out_shape=(out((OWN_ROWS,...]
where the time goes in v1:
time: 218 us; the launch traced here: 215 us
  Pallas kernels  201 us (92%)
  local copies, waits for them, and re-layouts  6.92 us (3%)
  other arithmetic  6.6 us (3%)
    pallas_call x1, Pallas kernels, run_step(): pl.pallas_call(partial(step_kernel, nz, rows), out_shape=(out((OWN_ROWS,...  201 us

profile of v1, /device:TPU:5, one launch (start us, length us, event | category | flops | bytes accessed | tf_op | source)
XLA Modules:
  0.0 214.9 jit_solution(12962202420247025194)
XLA Ops:
  0.6 1.0 slice_bitcast_fusion
  1.7 1.0 fusion.6
  2.6 0.9 concatenate.3.qo
  3.5 200.7 %layer_step.1 = (bf16[640,768]{1,0:T(8,128)(2,1)}, f32[640,768]{1,0:T(8,128)}, f32[3,96,768]{2,1,0:T(8,128)}, bf16[3,96,768]{2,1,0:T(8,128)(2,1)}, f32[2,8,768]{...) custom-call(s32[16]{0:T(128)} %tags.1, s32[16]{0:T(128)} %lens.1, ...), custom_call_target="tpu_custom_call" | custom-call | tf_op jit(solution)/shard_map/layer_step/pallas_call | solution.py:846
  204.2 1.4 fusion.1
  205.6 1.1 fusion.5
  206.8 0.0 copy-start.3
  206.8 0.0 copy-start
  206.8 0.3 reshape_squeeze.3
  207.1 0.3 slice.55
  207.4 0.1 copy.25
  207.5 0.8 copy.27
  208.3 0.9 copy.26
  209.2 0.0 copy-done.3
  209.2 0.1 dynamic-slice_compare_fusion
  209.3 0.1 broadcast_in_dim.19
  209.4 0.1 broadcast_in_dim.20
  209.5 0.0 copy-done
  209.5 0.0 copy-start.2
  209.5 2.9 %convert_select_fusion = f32[640,768]{1,0:T(8,128)} fusion(f32[640,768]{1,0:T(8,128)S(1)} %copy-done, bf16[640,768]{1,0:T(8,128)(2,1)} %get-tuple-element.18, pred[640]{0:T(1024)(128)(4,1)S(1)} %broadcast_in_dim.20), kind=kLoop, calls=%fused_computation.4 | loop fusion | flops 983040 | bytes 4915840 | tf_op jit(solution)/shard_map/jit(_where)/select_n | solution.py:918
  212.4 0.0 copy-done.1
  212.4 0.0 copy-done.2
  212.4 1.1 broadcast_select_fusion
  213.5 1.4 constant_dynamic-slice_fusion.1
  (1 shorter events, 0.0 us)
Async XLA Ops:
  206.8 2.5 %copy-start.3 = (s32[16]{0:T(128)S(1)}, s32[16]{0:T(128)}, u32[]{:S(2)}) copy-start(s32[16]{0:T(128)} %tags.1) | copy-start | bytes 196
  206.8 2.7 %copy-start = (f32[640,768]{1,0:T(8,128)S(1)}, f32[640,768]{1,0:T(8,128)}, u32[]{:S(2)}) copy-start(f32[640,768]{1,0:T(8,128)} %get-tuple-element.17) | copy-start | bytes 5898244
  209.5 2.9 %copy-start.1 = (bf16[640,768]{1,0:T(8,128)(2,1)S(1)}, bf16[640,768]{1,0:T(8,128)(2,1)}, u32[]{:S(2)}) copy-start(bf16[640,768]{1,0:T(8,128)(2,1)} %get-tuple-element.15) | copy-start | bytes 2949124
  209.5 2.9 %copy-start.2 = (bf16[640,768]{1,0:T(8,128)(2,1)S(1)}, bf16[640,768]{1,0:T(8,128)(2,1)}, u32[]{:S(2)}) copy-start(bf16[640,768]{1,0:T(8,128)(2,1)} %get-tuple-element.16) | copy-start | bytes 2949124

commit v2 on v1

--- a/solution.py
+++ b/solution.py
@@ -224,9 +224,8 @@
     pieces(i, piece)
 
 
-def back_heads(t, i, d_attn, wo, d_heads):
-    r = chunk_rows(i)
-    d_heads[t, r, :GW] = dot_nn(d_attn[r], wo[t]).astype(BF)
+def back_heads(t, d_attn, wo, d_heads):
+    d_heads[t, :, :GW] = dot_nn(d_attn[...], wo[t]).astype(BF)
 
 
 def back_attend(t, chains, proj, probs, d_heads):
@@ -284,10 +283,10 @@
 
 def step_kernel(nz, rows,
                 tags, lens, x_in, cot, qo, up, dn, gain, bias,
-                y_own, g_own, own_out, oth_out, n_out, y_back, g_back, r_c,
-                w, x, proj, probs, hout, wo, mid, n1, s1, mid_low, act, slope, d_ffn, gown, r_x, r_z,
+                y_out, g_out, qo_out, up_out, dn_out, n_out, y_back, g_back, r_c,
+                w, x, proj, probs, hout, wo, mid, n1, s1, mid_low, act, slope, d_ffn, gown, r_x, r_z, oth,
                 n_all, prm, ngrad, n_c, n_x, n_z,
-                load_s, io_s, stage_s,
+                load_s, io_s, stage_s, out_s,
                 ys_s, ys_r, zs_s, zs_r, xs_s, xs_r, cs_s, cs_r, ex_s, ex_r, na_s, na_r,
                 c_s, c_r, x_s, x_r, z_s, z_r, y_s, y_r, e_s, e_r, ng_s, ng_r):
     z, xc, y, c = place()
@@ -572,7 +571,7 @@
             act_on(remote(src, dst, e_s.at[i], e_r.at[i, c], diagonal))
 
     def y_copy(i):
-        return pltpu.make_async_copy(y_stage(i), y_own.at[pl.ds(i * CHUNK, CHUNK)], io_s.at[i])
+        return pltpu.make_async_copy(y_stage(i), y_out.at[pl.ds(i * CHUNK, CHUNK)], io_s.at[i])
 
     loop(
         N_CHUNK,
@@ -597,50 +596,82 @@
         arrived(r_c.at[m, g], c_r.at[m, g])
         fetch(m, g).start()
 
+    middle = jnp.logical_and(z > 0, z < nz - 1)
+
+    def target(k):
+        down = jnp.where(nz - 1 - k > z, nz - 1 - k, nz - 2 - k)
+        up = jnp.where(k < z, k, k + 1)
+        return jnp.where(k == nz - 1, z, jnp.where(z < nz // 2, down, up))
+
     def core_add(m, g):
         fetch(m, g).wait()
 
         def body(i):
-            dz = i // 2 + 1
-            zz = z_of(dz)
-            xx = lax.rem(xc + 1 + i, 2)
-            p = part(zz, xx)
+            p = part(target(i // 2), lax.rem(xc + 1 + i, 2))
             gown[m, g, p] = (gown[m, g, p].astype(F32) + act[2 * g + 1 - c, p].astype(F32)).astype(BF)
 
         loop(2 * nz, body)
-        for dz in range(1, nz + 1):
-            zz = z_of(dz)
+
+        def over(k):
+            zz = target(k)
             remote(gown.at[m, g, part(zz, 1 - xc)], r_x.at[m, g, zz], x_s.at[m, g, zz], x_r.at[m, g, zz], other_x).start()
+
+        loop(nz, over)
 
     def sum_event(q):
         m = 2 - q // (2 * nz)
         g = (q // nz) % 2
-        dz = q % nz + 1
-        zz = z_of(dz)
+        k = q % nz
+        zz = target(k)
         arrived(r_x.at[m, g, zz], x_r.at[m, g, zz])
         p = part(zz, xc)
         gown[m, g, p] = (gown[m, g, p].astype(F32) + r_x[m, g, zz].astype(F32)).astype(BF)
 
-        @pl.when(dz < nz)
+        joins = jnp.logical_and(k == 0, jnp.logical_not(middle))
+        waits = jnp.logical_and(k == 0, middle)
+        beside = jnp.where(z == 0, 1, nz - 2)
+        to = jnp.where(joins, beside, zz)
+        slot = jnp.where(joins, beside, z)
+
+        @pl.when(jnp.logical_and(k < nz - 1, jnp.logical_not(waits)))
         def _():
-            remote(gown.at[m, g, p], r_z.at[m, g, dz], z_s.at[m, g, dz], z_r.at[m, g, dz], {"z": zz}).start()
-
-    def own_copy(m):
-        return pltpu.make_async_copy(mid.at[pl.ds(OWN_ROWS + m * rows, rows)], own_out.at[m], io_s.at[3 + m])
+            remote(gown.at[m, g, p], r_z.at[m, g, slot], z_s.at[m, g, zz], z_r.at[m, g, slot], {"z": to}).start()
+
+        @pl.when(jnp.logical_and(k == jnp.where(m == 0, 1, nz - 2), middle))
+        def _():
+            far = target(0)
+            f = part(far, xc)
+            arrived(r_z.at[m, g, z], z_r.at[m, g, z])
+            gown[m, g, f] = (gown[m, g, f].astype(F32) + r_z[m, g, z].astype(F32)).astype(BF)
+            remote(gown.at[m, g, f], r_z.at[m, g, z], z_s.at[m, g, far], z_r.at[m, g, z], {"z": far}).start()
+
+    outs = (qo_out, up_out, dn_out)
+
+    def out_stage(m, other):
+        return mid.at[pl.ds(m * rows + (0 if other else OWN_ROWS), rows)]
+
+    def out_copy(m, other):
+        return pltpu.make_async_copy(out_stage(m, other), outs[m].at[1 - y if other else y], out_s.at[m, other])
 
     def last_send(m):
-        return remote(mid_low.at[pl.ds(EXT_ROWS + m * rows, rows)], oth_out.at[m], y_s.at[m], y_r.at[m], across)
+        return remote(mid_low.at[pl.ds(EXT_ROWS + m * rows, rows)], oth.at[m], y_s.at[m], y_r.at[m], across)
 
     def finish(m, g):
         total = gown[m, g, part(z, xc)].astype(F32)
         for dz in range(1, nz):
-            arrived(r_z.at[m, g, dz], z_r.at[m, g, dz])
-            total += r_z[m, g, dz].astype(F32)
+            source = z_of(dz)
+            direct = jnp.abs(source - z) < nz - 1
+
+            @pl.when(direct)
+            def _():
+                arrived(r_z.at[m, g, source], z_r.at[m, g, source])
+
+            total += jnp.where(direct, r_z[m, g, source].astype(F32), 0.0)
 
         @pl.when(y == g)
         def _():
-            mid[OWN_ROWS + m * rows : OWN_ROWS + (m + 1) * rows] = total
-            own_copy(m).start()
+            out_stage(m, 0)[...] = total
+            out_copy(m, 0).start()
 
         @pl.when(y != g)
         def _():
@@ -715,7 +746,7 @@
             act_on(remote(n_out.at[y], n_out.at[y], ng_s.at[nz + 1], ng_r.at[nz + 1], across))
 
     send_norms(0, start)
-    loop(GROUPS * N_CHUNK, lambda i: back_heads(i // N_CHUNK, i % N_CHUNK, d_ffn, wo, slope))
+    loop(GROUPS, lambda t: back_heads(t, d_ffn, wo, slope))
     sum_event(6)
     send_norms(0, recv)
     send_norms(0, lambda cp: cp.wait_send())
@@ -733,22 +764,22 @@
     seen = 7 + GROUPS * per // 2
 
     def qkv_grads(q):
-        g = q % 2
+        g, own = q // 2, q % 2
 
         def store(col, value):
             value = value.astype(BF)
 
-            @pl.when(q < 2)
+            @pl.when(own == 0)
             def _():
                 spare(0, g)[:, col : col + 128] = value
 
-            @pl.when(q >= 2)
+            @pl.when(own == 1)
             def _():
                 gown[0, g, :, col : col + 128] = value
 
-        grad_qkv_out(2 * g + jnp.where(q < 2, 1 - c, c), x, proj, d_ffn, hout, store)
-
-        @pl.when(q < 2)
+        grad_qkv_out(2 * g + jnp.where(own == 0, 1 - c, c), x, proj, d_ffn, hout, store)
+
+        @pl.when(own == 0)
         def _():
             core_send(0, g).start()
 
@@ -756,12 +787,14 @@
         4,
         qkv_grads,
         {
-            1: then((sum_event, seen)),
-            2: then((core_fetch, 0, 0), (core_fetch, 0, 1), (sum_event, seen + 1)),
-            3: then((core_add, 0, 0), (core_add, 0, 1), (sum_event, seen + 2)),
+            0: then((sum_event, seen)),
+            1: then((core_fetch, 0, 0), (sum_event, seen + 1)),
+            2: then((core_add, 0, 0), (sum_event, seen + 2)),
+            3: then((core_fetch, 0, 1), (core_add, 0, 1)),
         },
     )
     seen += 3
+
     def inputs_back(i):
         k = lax.rem(i + N_CHUNK - 1, N_CHUNK)
 
@@ -780,38 +813,72 @@
 
     weave(N_CHUNK, inputs_back, {1: then((sum_event, seen)), 2: then((sum_event, seen + 1))})
     seen += 2
-    g_copy = pltpu.make_async_copy(mid.at[pl.ds(0, OWN_ROWS)], g_own, io_s.at[2])
-    g_copy.start()
-    total_events = 6 * nz
     after = 4 * nz
     if seen < after:
         loop(after - seen, lambda q: sum_event(seen + q))
-        seen = after
     for g in range(2):
         finish(2, g)
-    loop(nz, lambda q: sum_event(after + q))
+    loop(2, lambda q: sum_event(after + q))
+
+    trips = [
+        pltpu.make_async_copy(g_back, proj.at[0, pl.ds(0, OWN_ROWS)], io_s.at[0]),
+        pltpu.make_async_copy(y_out, proj.at[1, pl.ds(0, OWN_ROWS)], io_s.at[1]),
+        pltpu.make_async_copy(y_back, proj.at[2, pl.ds(0, OWN_ROWS)], io_s.at[2]),
+    ]
+    y_again = pltpu.make_async_copy(proj.at[1, pl.ds(0, OWN_ROWS)], y_out, io_s.at[1])
+    g_copy = pltpu.make_async_copy(mid.at[pl.ds(0, OWN_ROWS)], g_out, io_s.at[3])
+
+    @pl.when(lender)
+    def _():
+        for i, dst in enumerate((y_back, g_back)):
+            for j in range(2):
+                arrived(dst.at[pl.ds(j * EXT_ROWS, EXT_ROWS)], e_r.at[i, j])
+        for cp in trips:
+            cp.start()
+        for cp in trips:
+            cp.wait()
+
+        def merge(s):
+            r = chunk_rows(s, LENGTH)
+            keep = jnp.zeros((LENGTH, D), F32) + mine(s) > 0.5
+            mid[r] = jnp.where(keep, mid[r], proj[0, r].astype(F32))
+            proj[1, r] = jnp.where(keep, proj[1, r].astype(F32), proj[2, r].astype(F32)).astype(BF)
+
+        loop(OWN, merge)
+        y_again.start()
+
+    g_copy.start()
+    loop(nz - 2, lambda q: sum_event(after + 2 + q))
     send_norms(1, recv)
     send_norms(1, lambda cp: cp.wait_send())
     n_x[...] += n_c[...]
     send_norms(2, start)
     for g in range(2):
         finish(1, g)
-    loop(nz, lambda q: sum_event(after + nz + q))
+    loop(nz - 1, lambda q: sum_event(after + nz + q))
     total = n_x[...]
     for dz in range(1, nz):
         arrived(n_z.at[dz], ng_r.at[1 + dz])
         total += n_z[dz]
     n_out[y] = total
     send_norms(3, start)
-    for g in range(2):
-        finish(0, g)
+    finish(0, 0)
+    sum_event(after + 2 * nz - 1)
+    finish(0, 1)
+    g_copy.wait()
+    for m in (2, 1, 0):
+        arrived(oth.at[m], y_r.at[m])
+        out_stage(m, 1)[...] = oth[m].astype(F32)
+        out_copy(m, 1).start()
 
     def sums_sent(i):
         m, g = i // 2, i % 2
-        for dz in range(nz):
-            if dz:
-                has_left(r_x.at[0, 0, 0], z_s.at[m, g, dz])
-            has_left(r_x.at[0, 0, 0], x_s.at[m, g, dz])
+        for zz in range(nz):
+            @pl.when(z != zz)
+            def _():
+                has_left(r_x.at[0, 0, 0], z_s.at[m, g, zz])
+
+            has_left(r_x.at[0, 0, 0], x_s.at[m, g, zz])
 
     loop(6, sums_sent)
     loop(6, gather_sent)
@@ -819,22 +886,20 @@
         core_send(0, g).wait_send()
     for m in range(3):
         has_left(mats[m].at[0], ys_s.at[m])
-        own_copy(m).wait()
-        last_send(m).wait()
+        for other in range(2):
+            out_copy(m, other).wait()
+        last_send(m).wait_send()
     lend(x_in, x, 0, lambda cp: cp.wait_send())
     lend(cot, d_ffn, 1, lambda cp: cp.wait_send())
     for i in range(4):
         norm_hop(i, lambda cp: cp.wait_send())
     send_norms(2, lambda cp: cp.wait_send())
     send_norms(3, lambda cp: cp.wait())
-    g_copy.wait()
     has_left(mid_low.at[pl.ds(0, EXT_ROWS)], e_s.at[1])
 
     @pl.when(lender)
     def _():
-        for i, dst in enumerate((y_back, g_back)):
-            for j in range(2):
-                arrived(dst.at[pl.ds(j * EXT_ROWS, EXT_ROWS)], e_r.at[i, j])
+        y_again.wait()
 
 
 def run_step(nz, tags, lens, x_in, cot, qo, up, dn, gain, bias):
@@ -848,15 +913,16 @@
         out_shape=(
             out((OWN_ROWS, D), BF),
             out((OWN_ROWS, D), F32),
-            out((3, rows, D), F32),
-            out((3, rows, D), BF),
+            out((2, rows, D), F32),
+            out((2, rows, D), F32),
+            out((2, rows, D), F32),
             out((2, 8, D), F32),
             out((OWN_ROWS, D), BF),
             out((OWN_ROWS, D), BF),
             out((3, 2, D, D), BF),
         ),
         in_specs=[S, S, ANY, ANY, ANY, ANY, ANY, V, V],
-        out_specs=(ANY, ANY, ANY, ANY, V, ANY, ANY, ANY),
+        out_specs=(ANY, ANY, ANY, ANY, ANY, V, ANY, ANY, ANY),
         scratch_shapes=[
             pltpu.VMEM((3, GROUPS, D, D), BF),
             pltpu.VMEM((ROWS, D), BF),
@@ -874,13 +940,14 @@
             pltpu.VMEM((3, 2, D, D), BF),
             pltpu.VMEM((3, 2, nz, rows, D), BF),
             pltpu.VMEM((3, 2, nz, rows, D), BF),
+            pltpu.VMEM((3, rows, D), BF),
             pltpu.VMEM((8 * nz, 8, 128), F32),
             pltpu.VMEM((8, D), F32),
             pltpu.VMEM((8, D), F32),
             pltpu.VMEM((8, D), F32),
             pltpu.VMEM((8, D), F32),
             pltpu.VMEM((nz, 8, D), F32),
-            sem((5,)), sem((6,)), sem((2,)),
+            sem((5,)), sem((4,)), sem((2,)), sem((3, 2)),
             sem((3,)), sem((3,)),
             sem((3, 2, 2, nz)), sem((3, 2, 2, nz)),
             sem((3, 2, nz)), sem((3, 2, nz)),
@@ -909,16 +976,10 @@
     for i in range(3):
         qo += [w_qkv[:, :, i], w_out[:, :, HEAD_DIM * i : HEAD_DIM * (i + 1)]]
     qo = jnp.concatenate(qo, -1)
-    y_own, g_own, own_g, oth_g, n_sum, y_back, g_back, _ = run_step(
+    y_out, x_grad, qo_grad, up_grad, down_grad, n_sum, _, _, _ = run_step(
         nz, tags, lengths, x_in, cotangent, qo, w_up, w_down, norm_gain, norm_bias
     )
-    kinds = lax.dynamic_slice_in_dim(tags, (2 * y + c) * OWN, OWN)
-    mine = jnp.repeat(kinds == y, LENGTH)[:, None]
-    y_out = jnp.where(mine, y_own, y_back)
-    x_grad = jnp.where(mine, g_own, g_back.astype(F32))
-    oth_g = oth_g.astype(F32)
-    both = jnp.stack([jnp.where(y == 0, own_g, oth_g), jnp.where(y == 0, oth_g, own_g)])
-    packed = both[:, 0].reshape(2, rows, 3, GW)
+    packed = qo_grad.reshape(2, rows, 3, GW)
     me = ((z * 2 + x) * 2 + y) * 2 + c
     n_mine = lax.dynamic_slice_in_dim(n_sum, me * cols, cols, 2)
     return (
@@ -926,8 +987,8 @@
         x_grad,
         packed[..., : GW - HEAD_DIM],
         packed[..., GW - HEAD_DIM :].reshape(w_out.shape),
-        both[:, 1],
-        both[:, 2],
+        up_grad,
+        down_grad,
         n_mine[:, :2],
         n_mine[:, 2:4],
     )
@@ -1199,7 +1260,7 @@
         P(None, None, ("dp", "tensor")),
     )
     n_dp, n_tensor = mesh.shape["dp"], mesh.shape["tensor"]
-    if n_tensor != GROUPS or n_dp not in (8, 16):
+    if n_tensor != GROUPS or n_dp != 8:
         return jax.shard_map(
             general_local, mesh=mesh, in_specs=placed, out_specs=results, check_vma=False
         )

time: 218 us -> 211 us (0.968); the launches traced: 215 us -> 211 us
  other arithmetic: 6.6 us -> 0 us
  local copies, waits for them, and re-layouts: 6.92 us -> 13.1 us
  Pallas kernels: 201 us -> 197 us
    unnamed x10 -> x12, local copies, waits for them, and re-layouts: 1.76 us -> 7.03 us
    select_n x2 -> x0, other arithmetic: 3.98 us -> none  [the longest x1 2.86 us: split_local(): x_grad = jnp.where(mine, g_own, g_back.astype(F32))]
    pallas_call x1, Pallas kernels: 201 us -> 197 us  [run_step(): pl.pallas_call(partial(step_kernel, nz, rows), out_shape=(out((OWN_ROWS,...]
where the time goes in v2:
time: 211 us
  Pallas kernels  197 us (93%)
  local copies, waits for them, and re-layouts  13.1 us (6%)
    pallas_call x1, Pallas kernels, run_step(): pl.pallas_call(partial(step_kernel, nz, rows), out_shape=(out((OWN_ROWS,...  197 us
    unnamed x12, local copies, waits for them, and re-layouts  7.03 us

profile of v2, /device:TPU:5, one launch (start us, length us, event | category | flops | bytes accessed | tf_op | source)
XLA Modules:
  0.0 210.8 jit_solution(11020241391398144078)
XLA Ops:
  0.6 1.0 slice_bitcast_fusion
  1.7 1.0 fusion
  2.6 0.9 concatenate.3.qo
  3.5 197.1 %layer_step.1 = (bf16[640,768]{1,0:T(8,128)(2,1)}, f32[640,768]{1,0:T(8,128)}, f32[2,96,768]{2,1,0:T(8,128)}, f32[2,96,768]{2,1,0:T(8,128)}, f32[2,96,768]{2,1,0...) custom-call(s32[16]{0:T(128)} %tags.1, s32[16]{0:T(128)} %lens.1, ...), custom_call_target="tpu_custom_call" | custom-call | tf_op jit(solution)/shard_map/layer_step/pallas_call | solution.py:911
  200.6 1.4 reshape.22
  201.9 0.9 copy.26
  202.9 0.0 copy-start
  202.9 0.3 slice.41
  203.1 0.1 copy.25
  203.3 0.8 copy.27
  204.1 1.4 constant_dynamic-slice_fusion.1
  205.5 2.2 %copy.35 = bf16[640,768]{1,0:T(8,128)(2,1)} copy(bf16[640,768]{1,0:T(8,128)(2,1)} %get-tuple-element.44) | data formatting | bytes 1966080
  207.7 0.0 copy-done
  207.7 0.0 copy-start.2
  207.7 0.0 copy-start.1
  207.7 1.3 copy.36
  209.0 0.2 copy-done.2
  209.2 0.8 copy.37
  210.0 0.0 copy-done.1
  210.0 0.8 copy.38
Async XLA Ops:
  202.9 4.9 %copy-start = (f32[640,768]{1,0:T(8,128)S(1)}, f32[640,768]{1,0:T(8,128)}, u32[]{:S(2)}) copy-start(f32[640,768]{1,0:T(8,128)} %get-tuple-element.45) | copy-start | bytes 5898244
  207.7 1.4 copy-start.2
  207.7 2.3 %copy-start.1 = (f32[2,96,768]{2,1,0:T(8,128)S(1)}, f32[2,96,768]{2,1,0:T(8,128)}, u32[]{:S(2)}) copy-start(f32[2,96,768]{2,1,0:T(8,128)} %get-tuple-element.49) | copy-start | bytes 1769476

commit v3 on v2

--- a/solution.py
+++ b/solution.py
@@ -282,9 +282,9 @@
 
 
 def step_kernel(nz, rows,
-                tags, lens, x_in, cot, qo, up, dn, gain, bias,
+                tags, lens, x_in, cot, qkv, wout, up, dn, gain, bias,
                 y_out, g_out, qo_out, up_out, dn_out, n_out, y_back, g_back, r_c,
-                w, x, proj, probs, hout, wo, mid, n1, s1, mid_low, act, slope, d_ffn, gown, r_x, r_z, oth,
+                w, x, proj, probs, hout, wo, mid, n1, s1, mid_low, act, slope, d_ffn, gown, r_x, r_z, oth, v_qkv, v_out, far,
                 n_all, prm, ngrad, n_c, n_x, n_z,
                 load_s, io_s, stage_s, out_s,
                 ys_s, ys_r, zs_s, zs_r, xs_s, xs_r, cs_s, cs_r, ex_s, ex_r, na_s, na_r,
@@ -292,7 +292,7 @@
     z, xc, y, c = place()
     core, across, other_x = {"c": 1 - c}, {"y": 1 - y}, {"x": 1 - xc}
     diagonal = {"y": 1 - y, "c": 1 - c}
-    mats = (qo, up, dn)
+    mats = (None, up, dn)
     lender = y != c
     home = (2 * y + c) * OWN
     away = (2 - y) * OWN + c * EXTRA
@@ -318,10 +318,12 @@
     def block(m, g, zz, xx):
         return w.at[m, group(g), part(zz, xx)]
 
-    loads = [pltpu.make_async_copy(mats[m].at[y], block(m, 0, z, xc), load_s.at[m]) for m in range(3)]
+    loads = [pltpu.make_async_copy(mats[m].at[y], block(m, 0, z, xc), load_s.at[m]) for m in range(1, 3)]
     loads += [
         pltpu.make_async_copy(x_in, x.at[pl.ds(0, OWN_ROWS)], load_s.at[3]),
         pltpu.make_async_copy(cot, d_ffn.at[pl.ds(0, OWN_ROWS)], load_s.at[4]),
+        pltpu.make_async_copy(qkv, v_qkv, load_s.at[0]),
+        pltpu.make_async_copy(wout, v_out, load_s.at[5]),
     ]
     for cp in loads:
         cp.start()
@@ -332,7 +334,22 @@
         n_all[me, 2 * i : 2 * i + 2, :cols] = gain[i]
         n_all[me, 4 + 2 * i : 6 + 2 * i, :cols] = bias[i]
     ngrad[...] = jnp.zeros_like(ngrad)
+    for cp in loads[4:]:
+        cp.wait()
+
+    def packed(k):
+        tail = v_out[k]
+        cols = []
+        for i in range(3):
+            cols += [v_qkv[k, i], tail[:, HEAD_DIM * i : HEAD_DIM * (i + 1)]]
+        return jnp.concatenate(cols, 1)
+
+    w[0, group(0), part(z, xc)] = packed(y)
+    far[...] = packed(1 - y)
     meet(nz, z, xc, y, c)
+
+    def given(m):
+        return mats[m].at[1 - y] if m else far
 
     def lend(arr, out, i, act_on):
         @pl.when(lender)
@@ -342,7 +359,7 @@
                 act_on(remote(src, out.at[pl.ds(OWN_ROWS, EXT_ROWS)], ex_s.at[i, j], ex_r.at[i], who))
 
     for m in range(3):
-        remote(mats[m].at[1 - y], w.at[m, group(0), part(z, xc)], ys_s.at[m], ys_r.at[m], across).start()
+        remote(given(m), w.at[m, group(0), part(z, xc)], ys_s.at[m], ys_r.at[m], across).start()
     lend(x_in, x, 0, lambda cp: cp.start())
     lend(cot, d_ffn, 1, lambda cp: cp.start())
 
@@ -448,8 +465,8 @@
             for dz in range(1, nz):
                 act_on(remote(ref, ref, na_s.at[2 + dz], na_r.at[2 + dz], {"z": z_of(dz)}))
 
-    for m in range(3):
-        loads[m].wait()
+    for cp in loads[:2]:
+        cp.wait()
     norm_hop(0, start)
     own_z(0)
     for g in range(2):
@@ -476,7 +493,7 @@
     norm_hop(2, recv)
     norm_hop(3, start)
     gathered(0)
-    loads[3].wait()
+    loads[2].wait()
     arrived(x.at[pl.ds(OWN_ROWS, EXT_ROWS)], ex_r.at[0])
 
     def projection(i):
@@ -553,7 +570,7 @@
     for j in range(2, nz):
         x_event(2, j, 1, 2)
     gathered(2, 1, 2)
-    loads[4].wait()
+    loads[3].wait()
     arrived(d_ffn.at[pl.ds(OWN_ROWS, EXT_ROWS)], ex_r.at[1])
 
     def y_stage(i):
@@ -885,7 +902,7 @@
     for g in range(2):
         core_send(0, g).wait_send()
     for m in range(3):
-        has_left(mats[m].at[0], ys_s.at[m])
+        has_left(given(m), ys_s.at[m])
         for other in range(2):
             out_copy(m, other).wait()
         last_send(m).wait_send()
@@ -902,7 +919,7 @@
         y_again.wait()
 
 
-def run_step(nz, tags, lens, x_in, cot, qo, up, dn, gain, bias):
+def run_step(nz, tags, lens, x_in, cot, qkv, wout, up, dn, gain, bias):
     rows = up.shape[1]
     V = pl.BlockSpec(memory_space=pltpu.VMEM)
     S = pl.BlockSpec(memory_space=pltpu.SMEM)
@@ -921,7 +938,7 @@
             out((OWN_ROWS, D), BF),
             out((3, 2, D, D), BF),
         ),
-        in_specs=[S, S, ANY, ANY, ANY, ANY, ANY, V, V],
+        in_specs=[S, S] + [ANY] * 6 + [V, V],
         out_specs=(ANY, ANY, ANY, ANY, ANY, V, ANY, ANY, ANY),
         scratch_shapes=[
             pltpu.VMEM((3, GROUPS, D, D), BF),
@@ -941,13 +958,16 @@
             pltpu.VMEM((3, 2, nz, rows, D), BF),
             pltpu.VMEM((3, 2, nz, rows, D), BF),
             pltpu.VMEM((3, rows, D), BF),
+            pltpu.VMEM(qkv.shape, BF),
+            pltpu.VMEM(wout.shape, BF),
+            pltpu.VMEM((rows, D), BF),
             pltpu.VMEM((8 * nz, 8, 128), F32),
             pltpu.VMEM((8, D), F32),
             pltpu.VMEM((8, D), F32),
             pltpu.VMEM((8, D), F32),
             pltpu.VMEM((8, D), F32),
             pltpu.VMEM((nz, 8, D), F32),
-            sem((5,)), sem((4,)), sem((2,)), sem((3, 2)),
+            sem((6,)), sem((4,)), sem((2,)), sem((3, 2)),
             sem((3,)), sem((3,)),
             sem((3, 2, 2, nz)), sem((3, 2, 2, nz)),
             sem((3, 2, nz)), sem((3, 2, nz)),
@@ -965,33 +985,80 @@
             collective_id=0, has_side_effects=True, vmem_limit_bytes=67043328
         ),
         name="layer_step",
-    )(tags, lens, x_in, cot, qo, up, dn, gain, bias)
+    )(tags, lens, x_in, cot, qkv, wout, up, dn, gain, bias)
+
+
+def deliver_kernel(cols, y_in, g_in, qo, up_in, dn_in, sums,
+                   y_out, g_out, qkv_out, wout_out, up_out, dn_out, gain_out, bias_out,
+                   v_y, v_g, v_qo, v_up, v_dn, v_qkv, v_out, in_s, out_s):
+    through = [(up_in, v_up, up_out), (dn_in, v_dn, dn_out)]
+    for k in range(OWN):
+        r = pl.ds(k * LENGTH, LENGTH)
+        through.append((g_in.at[r], v_g.at[r], g_out.at[r]))
+    for k in range(2):
+        r = pl.ds(k * CHUNK, CHUNK)
+        through.append((y_in.at[r], v_y.at[r], y_out.at[r]))
+    n = len(through)
+    first = pltpu.make_async_copy(qo, v_qo, in_s.at[n])
+    first.start()
+    loads, stores = [], []
+    for i, (src, via, dst) in enumerate(through):
+        loads.append(pltpu.make_async_copy(src, via, in_s.at[i]))
+        stores.append(pltpu.make_async_copy(via, dst, out_s.at[i]))
+        loads[-1].start()
+    z, x, y, c = place()
+    me = ((z * 2 + x) * 2 + y) * 2 + c
+    for k in range(2):
+        turned = pltpu.roll(sums[k], lax.rem(D - me * cols, D), 1)
+        gain_out[k] = turned[0:2, :cols]
+        bias_out[k] = turned[2:4, :cols]
+    first.wait()
+    for k in range(2):
+        tail = []
+        for i in range(3):
+            v_qkv[k, i] = v_qo[k, :, GW * i : GW * i + GW - HEAD_DIM]
+            tail.append(v_qo[k, :, GW * (i + 1) - HEAD_DIM : GW * (i + 1)])
+        v_out[k] = jnp.concatenate(tail, 1)
+    stores.append(pltpu.make_async_copy(v_qkv, qkv_out, out_s.at[n]))
+    stores.append(pltpu.make_async_copy(v_out, wout_out, out_s.at[n + 1]))
+    for i in range(n):
+        loads[i].wait()
+        stores[i].start()
+    for cp in stores[n:]:
+        cp.start()
+    for cp in stores:
+        cp.wait()
+
+
+def deliver(cols, y_in, g_in, qo, up_in, dn_in, sums):
+    rows = qo.shape[1]
+    V = pl.BlockSpec(memory_space=pltpu.VMEM)
+    sem = pltpu.SemaphoreType.DMA
+    out = jax.ShapeDtypeStruct
+    width = GW - HEAD_DIM
+    shapes = [((2, 3, rows, width), F32), ((2, rows, width), F32)]
+    whole = [(y_in.shape, BF), (g_in.shape, F32), (qo.shape, F32), (qo.shape, F32), (qo.shape, F32)]
+    return pl.pallas_call(
+        partial(deliver_kernel, cols),
+        out_shape=tuple(
+            out(*p) for p in whole[:2] + shapes + whole[3:] + [((2, 2, cols), F32)] * 2
+        ),
+        in_specs=[ANY] * 5 + [V],
+        out_specs=(ANY,) * 6 + (V, V),
+        scratch_shapes=[pltpu.VMEM(*p) for p in whole + shapes] + [sem((9,)), sem((10,))],
+        name="deliver",
+    )(y_in, g_in, qo, up_in, dn_in, sums)
 
 
 def split_local(nz, x_in, tags, lengths, w_qkv, w_out, w_up, w_down, norm_gain, norm_bias, cotangent):
-    z, x, y, c = place()
-    rows = w_up.shape[1]
     cols = norm_gain.shape[2]
-    qo = []
-    for i in range(3):
-        qo += [w_qkv[:, :, i], w_out[:, :, HEAD_DIM * i : HEAD_DIM * (i + 1)]]
-    qo = jnp.concatenate(qo, -1)
     y_out, x_grad, qo_grad, up_grad, down_grad, n_sum, _, _, _ = run_step(
-        nz, tags, lengths, x_in, cotangent, qo, w_up, w_down, norm_gain, norm_bias
-    )
-    packed = qo_grad.reshape(2, rows, 3, GW)
-    me = ((z * 2 + x) * 2 + y) * 2 + c
-    n_mine = lax.dynamic_slice_in_dim(n_sum, me * cols, cols, 2)
-    return (
-        y_out,
-        x_grad,
-        packed[..., : GW - HEAD_DIM],
-        packed[..., GW - HEAD_DIM :].reshape(w_out.shape),
-        up_grad,
-        down_grad,
-        n_mine[:, :2],
-        n_mine[:, 2:4],
-    )
+        nz, tags, lengths, x_in, cotangent, w_qkv.transpose(0, 2, 1, 3), w_out, w_up, w_down, norm_gain, norm_bias
+    )
+    y_out, x_grad, qkv, out, up, down, gain, bias = deliver(
+        cols, y_out, x_grad, qo_grad, up_grad, down_grad, n_sum
+    )
+    return y_out, x_grad, qkv.transpose(0, 2, 1, 3), out, up, down, gain, bias
 
 
 def typed_map(operand, stacked, chain_kinds, pattern):

time: 211 us -> 205 us (0.972)
  local copies, waits for them, and re-layouts: 13.1 us -> 0 us
  Pallas kernels: 197 us -> 204 us
    unnamed x12 -> x0, local copies, waits for them, and re-layouts: 7.03 us -> none
    pallas_call x0 -> x1, Pallas kernels: none -> 5.29 us  [deliver(): pl.pallas_call(partial(deliver_kernel, cols), out_shape=tuple((out(*p) fo...]
    slice x4 -> x0, local copies, waits for them, and re-layouts: 2.8 us -> none  [the longest x1 1.45 us: split_local(): n_mine[:, 2:4]]
where the time goes in v3:
time: 205 us
  Pallas kernels  204 us (100%)
    pallas_call x1, Pallas kernels, run_step(): pl.pallas_call(partial(step_kernel, nz, rows), out_shape=(out((OWN_ROWS,...  199 us
    pallas_call x1, Pallas kernels, deliver(): pl.pallas_call(partial(deliver_kernel, cols), out_shape=tuple((out(*p) fo...  5.29 us

profile of v3, /device:TPU:5, one launch (start us, length us, event | category | flops | bytes accessed | tf_op | source)
XLA Modules:
  0.0 204.8 jit_solution(15397182782202687725)
XLA Ops:
  0.6 198.7 %layer_step.1 = (bf16[640,768]{1,0:T(8,128)(2,1)}, f32[640,768]{1,0:T(8,128)}, f32[2,96,768]{2,1,0:T(8,128)}, f32[2,96,768]{2,1,0:T(8,128)}, f32[2,96,768]{2,1,0...) custom-call(s32[16]{0:T(128)} %tags.1, s32[16]{0:T(128)} %lens.1, ...), custom_call_target="tpu_custom_call" | custom-call | tf_op jit(solution)/shard_map/layer_step/pallas_call | solution.py:928
  199.3 5.3 %deliver.1 = (bf16[640,768]{1,0:T(8,128)(2,1)}, f32[640,768]{1,0:T(8,128)}, f32[2,3,96,192]{3,2,1,0:T(8,128)}, f32[2,96,192]{2,1,0:T(8,128)}, f32[2,96,768]{2,1,...) custom-call(bf16[640,768]{1,0:T(8,128)(2,1)} %get-tuple-element.22.y_in, ...), custom_call_target="tpu_custom_call" | custom-call | tf_op jit(solution)/shard_map/deliver/pallas_call | solution.py:1041

commit v4 on v3

--- a/solution.py
+++ b/solution.py
@@ -267,6 +267,39 @@
     out(r, grad)
 
 
+MIXED = (2, 1)
+GATHER_FIRST = (
+    ('X', 0, 0), ('L', 0, 0), ('y', 0), ('X', 0, 1), ('L', 0, 1),
+    ('z', 0, 0, 1), ('z', 0, 1, 1), ('z', 0, 0, 2), ('x', 0, 0, 0), ('z', 0, 1, 2),
+    ('z', 0, 0, 3), ('y', 1), ('L', 1, 1), ('x', 0, 1, 1), ('z', 0, 1, 3),
+    ('x', 0, 1, 0), ('y', 2), ('X', 2, 1), ('L', 1, 0), ('X', 1, 0),
+    ('x', 0, 0, 2), ('X', 1, 1), ('z', 1, 1, 1), ('x', 0, 0, 3), ('L', 2, 0),
+    ('x', 0, 0, 1), ('x', 0, 1, 2), ('x', 0, 1, 3), ('z', 1, 0, 1),
+)
+GATHER_QKV = {
+    6: (('z', 1, 1, 2),),
+    11: (('z', 1, 0, 2),),
+}
+GATHER_ATTEND = {
+    2: (('x', 2, 1, 0),),
+    3: (('x', 1, 1, 1), ('x', 1, 0, 0), ('z', 1, 0, 3),),
+    4: (('L', 2, 1), ('z', 1, 1, 3), ('x', 1, 1, 0),),
+    5: (('z', 2, 0, 1), ('X', 2, 0),),
+}
+GATHER_NORM = {
+    0: (('z', 2, 1, 1),),
+    1: (('x', 1, 0, 3), ('x', 1, 0, 1), ('x', 1, 1, 2), ('x', 1, 0, 2), ('x', 1, 1, 3),),
+    2: (('z', 2, 0, 2),),
+}
+GATHER_UP = {
+    3: (('z', 2, 1, 2),),
+    5: (('z', 2, 0, 3),),
+    8: (('x', 2, 0, 1),),
+    10: (('x', 2, 0, 0), ('x', 2, 0, 2), ('x', 2, 0, 3),),
+    11: (('z', 2, 1, 3),),
+}
+
+
 def remote(src, dst, s_sem, r_sem, who):
     return pltpu.make_async_remote_copy(
         src_ref=src, dst_ref=dst, send_sem=s_sem, recv_sem=r_sem, device_id=who, device_id_type=MESH
@@ -287,7 +320,7 @@
                 w, x, proj, probs, hout, wo, mid, n1, s1, mid_low, act, slope, d_ffn, gown, r_x, r_z, oth, v_qkv, v_out, far,
                 n_all, prm, ngrad, n_c, n_x, n_z,
                 load_s, io_s, stage_s, out_s,
-                ys_s, ys_r, zs_s, zs_r, xs_s, xs_r, cs_s, cs_r, ex_s, ex_r, na_s, na_r,
+                ys_s, ys_r, zs_s, zs_r, zm_s, zm_r, xs_s, xs_r, cs_s, cs_r, ex_s, ex_r, na_s, na_r,
                 c_s, c_r, x_s, x_r, z_s, z_r, y_s, y_r, e_s, e_r, ng_s, ng_r):
     z, xc, y, c = place()
     core, across, other_x = {"c": 1 - c}, {"y": 1 - y}, {"x": 1 - xc}
@@ -372,12 +405,13 @@
     def recv(cp):
         cp.wait_recv()
 
-    def hop(m, g, d, j, ref, act_on):
+    def hop(m, g, d, j, ref, act_on, col=0):
         to = z + 1 - 2 * d
+        sems = (zm_s.at[d, j], zm_r.at[d, j]) if col else (zs_s.at[m, g, d, j], zs_r.at[m, g, d, j])
 
         @pl.when(jnp.logical_and(inside(to), j < nz))
         def _():
-            act_on(remote(ref, ref, zs_s.at[m, g, d, j], zs_r.at[m, g, d, j], {"z": to}))
+            act_on(remote(ref, ref, *sems, {"z": to}))
 
     def x_copy(m, g, zz):
         ref = block(m, g, zz, xc)
@@ -387,47 +421,58 @@
         ref = block(m, g, zz, xx)
         return remote(ref, ref, cs_s.at[m, g, zz, xx], cs_r.at[m, g, zz, xx], core)
 
-    def own_z(m):
-        def body(g):
-            @pl.when(g == 1)
-            def _():
-                arrived(block(m, 1, z, xc), ys_r.at[m])
-
-            for d in range(2):
-                hop(m, g, d, 1, block(m, g, z, xc), start)
-
-        loop(2, body)
+    def from_y(m):
+        arrived(block(m, 1, z, xc), ys_r.at[m])
+
+    def own_z(m, g):
+        for d in range(2):
+            hop(m, g, d, 1, block(m, g, z, xc), start)
 
     def own_xc(m, g):
         x_copy(m, g, z).start()
         c_copy(m, g, z, xc).start()
 
-    def z_event(m, j, first=0, last=2):
-        def body(q):
-            g, d = first + q // 2, q % 2
+    def z_event(m, g, j):
+        mixed = (m, g) == MIXED
+
+        def body(d):
             zz = z - j + 2 * j * d
 
             @pl.when(inside(zz))
             def _():
-                ref = block(m, g, zz, xc)
-                arrived(ref, zs_r.at[m, g, d, j])
-                hop(m, g, d, j + 1, ref, start)
-                x_copy(m, g, zz).start()
-                c_copy(m, g, zz, xc).start()
-
-        loop(2 * (last - first), body)
-
-    def x_event(m, j, first=0, last=2):
-        def body(q):
-            g, d = first + q // 2, q % 2
+                for col in range(2 if mixed else 1):
+                    ref = block(m, g, zz, lax.rem(xc + col, 2))
+                    arrived(ref, zm_r.at[d, j] if col else zs_r.at[m, g, d, j])
+                    hop(m, g, d, j + 1, ref, start, col)
+                    if not mixed:
+                        x_copy(m, g, zz).start()
+                    c_copy(m, g, zz, lax.rem(xc + col, 2)).start()
+
+        loop(2, body)
+
+    def x_event(m, g, j):
+        def body(d):
             zz = z - j + 2 * j * d
 
-            @pl.when(jnp.logical_and(inside(zz), j + 1 > d))
+            @pl.when(inside(zz))
             def _():
-                arrived(block(m, g, zz, 1 - xc), xs_r.at[m, g, zz])
+                ref = block(m, g, zz, 1 - xc)
+                arrived(ref, xs_r.at[m, g, zz])
+                if (m, g) == MIXED:
+                    for way in range(2):
+                        hop(m, g, way, 1, ref, start, 1)
                 c_copy(m, g, zz, 1 - xc).start()
 
-        loop(2 * (last - first), body)
+        loop(2 if j else 1, body)
+
+    kinds = {"y": from_y, "L": own_z, "X": own_xc, "z": z_event, "x": x_event}
+
+    def gather_steps(plan):
+        def run(steps):
+            for kind, *args in steps:
+                kinds[kind](*args)
+
+        return {k: partial(run, steps) for k, steps in plan.items()}
 
     def gathered(m, first=0, last=2):
         def body(i):
@@ -441,13 +486,21 @@
     def gather_sent(i):
         m, g = i // 2, i % 2
         ref = w.at[0, 0, pl.ds(0, rows)]
+        mixed = i == 2 * MIXED[0] + MIXED[1]
         for j in range(1, nz):
             for d in range(2):
                 @pl.when(inside(z - (1 - 2 * d) * (j - 1)))
                 def _():
                     hop(m, g, d, j, ref, lambda cp: cp.wait_send())
+
+                    @pl.when(mixed)
+                    def _():
+                        hop(m, g, d, j, ref, lambda cp: cp.wait_send(), 1)
         for zz in range(nz):
-            has_left(ref, xs_s.at[m, g, zz])
+            @pl.when(jnp.logical_or(jnp.logical_not(mixed), z == zz))
+            def _():
+                has_left(ref, xs_s.at[m, g, zz])
+
             for xx in range(2):
                 has_left(ref, cs_s.at[m, g, zz, xx])
 
@@ -468,28 +521,14 @@
     for cp in loads[:2]:
         cp.wait()
     norm_hop(0, start)
-    own_z(0)
-    for g in range(2):
-        own_xc(0, g)
-    z_event(0, 1)
-    norm_hop(0, recv)
-    norm_hop(1, start)
-    for j in range(2, nz):
-        z_event(0, j)
-        if j == 2:
-            own_z(1)
-    if nz < 3:
-        own_z(1)
-    norm_hop(1, recv)
-    norm_hop(2, start)
-    for g in range(2):
-        own_xc(1, g)
-    x_event(0, 0)
-    x_event(0, 1)
-    for j in range(1, nz - 1):
-        z_event(1, j)
-        x_event(0, j + 1)
-    own_z(2)
+    for kind, *args in GATHER_FIRST:
+        kinds[kind](*args)
+        if (kind, *args) == ("z", 0, 0, 1):
+            norm_hop(0, recv)
+            norm_hop(1, start)
+        if (kind, *args) == ("z", 0, 0, 3):
+            norm_hop(1, recv)
+            norm_hop(2, start)
     norm_hop(2, recv)
     norm_hop(3, start)
     gathered(0)
@@ -505,25 +544,13 @@
         def _():
             out_columns(t, w, wo)
 
-    def more_own():
-        z_event(1, nz - 1)
-        own_xc(2, 0)
-
-    weave(
-        GROUPS * N_CHUNK,
-        projection,
-        {0: more_own, 8: lambda: x_event(1, 0), 11: lambda: z_event(2, 1, 0, 1)},
-    )
+    weave(GROUPS * N_CHUNK, projection, gather_steps(GATHER_QKV))
     per = SLOTS // PAIR
 
     def attention(i):
         attend(i // per, [(i % per) * PAIR + k for k in range(PAIR)], length_of, proj, probs, hout)
 
-    weave(
-        GROUPS * per,
-        attention,
-        {2: lambda: x_event(1, 1), 3: lambda: z_event(2, 2, 0, 1), 7: lambda: x_event(1, 2)},
-    )
+    weave(GROUPS * per, attention, gather_steps(GATHER_ATTEND))
     norm_hop(3, recv)
     lane = lanes((2, D))
     gains, shifts = jnp.zeros((2, D), F32), jnp.zeros((2, D), F32)
@@ -539,36 +566,21 @@
                 shifts += piece
     prm[0:2] = gains
     prm[2:4] = shifts
-    loop(N_CHUNK, lambda i: first_norm(i, x, hout, wo, prm, mid, n1, s1, mid_low))
-    for j in range(3, nz):
-        z_event(2, j, 0, 1)
-        x_event(1, j)
-    own_xc(2, 1)
+    weave(
+        N_CHUNK,
+        lambda i: first_norm(i, x, hout, wo, prm, mid, n1, s1, mid_low),
+        gather_steps(GATHER_NORM),
+    )
     gathered(1)
     weave(
         GROUPS * N_CHUNK,
         lambda i: feed_up(i // N_CHUNK, i % N_CHUNK, mid_low, w, act, slope),
-        {
-            0: lambda: z_event(2, 1, 1, 2),
-            2: lambda: x_event(2, 0, 0, 1),
-            4: lambda: z_event(2, 2, 1, 2),
-            7: lambda: x_event(2, 1, 0, 1),
-        },
-    )
-    for j in range(2, nz):
-        if j > 2:
-            z_event(2, j, 1, 2)
-        x_event(2, j, 0, 1)
+        gather_steps(GATHER_UP),
+    )
     gathered(2, 0, 1)
     first_two = 2 * y
     last_two = 2 - first_two
-    weave(
-        N_CHUNK,
-        lambda i: feed_down(i, first_two, act, w, mid),
-        {0: lambda: x_event(2, 0, 1, 2), 2: lambda: x_event(2, 1, 1, 2)},
-    )
-    for j in range(2, nz):
-        x_event(2, j, 1, 2)
+    loop(N_CHUNK, lambda i: feed_down(i, first_two, act, w, mid))
     gathered(2, 1, 2)
     loads[3].wait()
     arrived(d_ffn.at[pl.ds(OWN_ROWS, EXT_ROWS)], ex_r.at[1])
@@ -970,6 +982,7 @@
             sem((6,)), sem((4,)), sem((2,)), sem((3, 2)),
             sem((3,)), sem((3,)),
             sem((3, 2, 2, nz)), sem((3, 2, 2, nz)),
+            sem((2, nz)), sem((2, nz)),
             sem((3, 2, nz)), sem((3, 2, nz)),
             sem((3, 2, nz, 2)), sem((3, 2, nz, 2)),
             sem((2, 2)), sem((2,)),

time: 205 us -> 201 us (0.980)
  Pallas kernels: 204 us -> 200 us
    pallas_call x1, Pallas kernels: 199 us -> 194 us  [run_step(): pl.pallas_call(partial(step_kernel, nz, rows), out_shape=(out((OWN_ROWS,...]
where the time goes in v4:
time: 201 us
  Pallas kernels  200 us (100%)
    pallas_call x1, Pallas kernels, run_step(): pl.pallas_call(partial(step_kernel, nz, rows), out_shape=(out((OWN_ROWS,...  194 us
    pallas_call x1, Pallas kernels, deliver(): pl.pallas_call(partial(deliver_kernel, cols), out_shape=tuple((out(*p) fo...  5.29 us

profile of v4, /device:TPU:5, one launch (start us, length us, event | category | flops | bytes accessed | tf_op | source)
XLA Modules:
  0.0 200.5 jit_solution(6928018025698477174)
XLA Ops:
  0.6 194.4 %layer_step.1 = (bf16[640,768]{1,0:T(8,128)(2,1)}, f32[640,768]{1,0:T(8,128)}, f32[2,96,768]{2,1,0:T(8,128)}, f32[2,96,768]{2,1,0:T(8,128)}, f32[2,96,768]{2,1,0...) custom-call(s32[16]{0:T(128)} %tags.1, s32[16]{0:T(128)} %lens.1, ...), custom_call_target="tpu_custom_call" | custom-call | tf_op jit(solution)/shard_map/layer_step/pallas_call | solution.py:940
  195.1 5.3 %deliver.1 = (bf16[640,768]{1,0:T(8,128)(2,1)}, f32[640,768]{1,0:T(8,128)}, f32[2,3,96,192]{3,2,1,0:T(8,128)}, f32[2,96,192]{2,1,0:T(8,128)}, f32[2,96,768]{2,1,...) custom-call(bf16[640,768]{1,0:T(8,128)(2,1)} %get-tuple-element.22.y_in, ...), custom_call_target="tpu_custom_call" | custom-call | tf_op jit(solution)/shard_map/deliver/pallas_call | solution.py:1054

commit v5 on v4

--- a/solution.py
+++ b/solution.py
@@ -36,13 +36,13 @@
     return tuple(lax.axis_index(a) for a in AXES)
 
 
-def meet(nz, z, x, y, c):
+def greet(nz, z, x, y, c):
     barrier = pltpu.get_barrier_semaphore()
     friends = [{"c": 1 - c}, {"y": 1 - y}, {"y": 1 - y, "c": 1 - c}, {"x": 1 - x}]
     friends += [{"z": lax.rem(z + dz, nz)} for dz in range(1, nz)]
     for friend in friends:
         pl.semaphore_signal(barrier, inc=1, device_id=friend, device_id_type=MESH)
-    pl.semaphore_wait(barrier, len(friends))
+    return barrier, len(friends)
 
 
 CHUNK = 320
@@ -317,11 +317,11 @@
 def step_kernel(nz, rows,
                 tags, lens, x_in, cot, qkv, wout, up, dn, gain, bias,
                 y_out, g_out, qo_out, up_out, dn_out, n_out, y_back, g_back, r_c,
-                w, x, proj, probs, hout, wo, mid, n1, s1, mid_low, act, slope, d_ffn, gown, r_x, r_z, oth, v_qkv, v_out, far,
+                w, x, proj, probs, hout, wo, mid, n1, s1, mid_low, act, slope, d_ffn, gown, r_xz, oth, v_qkv, v_out, far,
                 n_all, prm, ngrad, n_c, n_x, n_z,
                 load_s, io_s, stage_s, out_s,
                 ys_s, ys_r, zs_s, zs_r, zm_s, zm_r, xs_s, xs_r, cs_s, cs_r, ex_s, ex_r, na_s, na_r,
-                c_s, c_r, x_s, x_r, z_s, z_r, y_s, y_r, e_s, e_r, ng_s, ng_r):
+                c_s, c_r, cp_s, cp_r, x_s, x_r, z_s, z_r, y_s, y_r, e_s, e_r, ng_s, ng_r):
     z, xc, y, c = place()
     core, across, other_x = {"c": 1 - c}, {"y": 1 - y}, {"x": 1 - xc}
     diagonal = {"y": 1 - y, "c": 1 - c}
@@ -360,6 +360,7 @@
     ]
     for cp in loads:
         cp.start()
+    barrier, friends = greet(nz, z, xc, y, c)
     me = ((z * 2 + xc) * 2 + y) * 2 + c
     cols = gain.shape[2]
     n_all[me] = jnp.zeros((8, 128), F32)
@@ -379,7 +380,7 @@
 
     w[0, group(0), part(z, xc)] = packed(y)
     far[...] = packed(1 - y)
-    meet(nz, z, xc, y, c)
+    pl.semaphore_wait(barrier, friends)
 
     def given(m):
         return mats[m].at[1 - y] if m else far
@@ -586,7 +587,7 @@
     arrived(d_ffn.at[pl.ds(OWN_ROWS, EXT_ROWS)], ex_r.at[1])
 
     def y_stage(i):
-        return gown.at[1, i // 2, pl.ds(pl.multiple_of((i % 2) * CHUNK, CHUNK), CHUNK)]
+        return r_xz.at[i // 2, 0, pl.ds(pl.multiple_of((i % 2) * CHUNK, CHUNK), CHUNK)]
 
     def give_back(src, dst, i, act_on):
         dst = dst.at[pl.ds(pl.multiple_of(c * EXT_ROWS, EXT_ROWS), EXT_ROWS)]
@@ -612,18 +613,29 @@
         y_copy(i).start()
     give_back(y_stage(2), y_back, 0, start)
 
+    def x_place(m, g, i):
+        return r_xz.at[0, m, pl.ds(pl.multiple_of((g * nz + i) * rows, rows), rows)]
+
+    def z_place(m, g, i):
+        return r_xz.at[1, m, pl.ds(pl.multiple_of((g * nz + i) * rows, rows), rows)]
+
     def spare(m, g):
         return gown.at[0, g] if m else act.at[2 * g + c, pl.ds(0, D)]
 
     def core_send(m, g):
-        return remote(spare(m, g), r_c.at[m, g], c_s.at[m, g], c_r.at[m, g], core)
-
-    def fetch(m, g):
-        return pltpu.make_async_copy(r_c.at[m, g], act.at[2 * g + 1 - c, pl.ds(0, D)], stage_s.at[g])
-
-    def core_fetch(m, g):
-        arrived(r_c.at[m, g], c_r.at[m, g])
-        fetch(m, g).start()
+        there = r_c.at[g] if m else spare(0, g)
+        return remote(spare(m, g), there, c_s.at[m, g], c_r.at[m, g], core)
+
+    def fetch(g):
+        return pltpu.make_async_copy(r_c.at[g], act.at[2 * g + 1 - c, pl.ds(0, D)], stage_s.at[g])
+
+    def core_piece(g, k):
+        cols = pl.ds(k * GW, GW)
+        return remote(gown.at[0, g, :, cols], gown.at[1, g, :, cols], cp_s.at[g, k], cp_r.at[g, k], core)
+
+    def core_fetch(g):
+        arrived(r_c.at[g], c_r.at[1, g])
+        fetch(g).start()
 
     middle = jnp.logical_and(z > 0, z < nz - 1)
 
@@ -633,28 +645,38 @@
         return jnp.where(k == nz - 1, z, jnp.where(z < nz // 2, down, up))
 
     def core_add(m, g):
-        fetch(m, g).wait()
-
-        def body(i):
-            p = part(target(i // 2), lax.rem(xc + 1 + i, 2))
-            gown[m, g, p] = (gown[m, g, p].astype(F32) + act[2 * g + 1 - c, p].astype(F32)).astype(BF)
-
-        loop(2 * nz, body)
+        if m == 2:
+            for k in range(D // GW):
+                core_piece(g, k).wait_recv()
+            from_core = gown.at[1, g]
+        else:
+            from_core = act.at[2 * g + 1 - c, pl.ds(0, D)]
+            if m == 1:
+                fetch(g).wait()
+            else:
+                arrived(from_core, c_r.at[0, g])
+
+        def add(i):
+            p = part(target(i % nz), lax.rem(xc + 1 + i // nz, 2))
+            gown[m, g, p] += from_core[p]
 
         def over(k):
             zz = target(k)
-            remote(gown.at[m, g, part(zz, 1 - xc)], r_x.at[m, g, zz], x_s.at[m, g, zz], x_r.at[m, g, zz], other_x).start()
-
+            remote(gown.at[m, g, part(zz, 1 - xc)], x_place(m, g, zz), x_s.at[m, g, zz], x_r.at[m, g, zz], other_x).start()
+
+        loop(nz + 1, add)
         loop(nz, over)
+        loop(nz - 1, lambda i: add(nz + 1 + i))
 
     def sum_event(q):
         m = 2 - q // (2 * nz)
         g = (q // nz) % 2
         k = q % nz
         zz = target(k)
-        arrived(r_x.at[m, g, zz], x_r.at[m, g, zz])
+        over = x_place(m, g, zz)
+        arrived(over, x_r.at[m, g, zz])
         p = part(zz, xc)
-        gown[m, g, p] = (gown[m, g, p].astype(F32) + r_x[m, g, zz].astype(F32)).astype(BF)
+        gown[m, g, p] += over[...]
 
         joins = jnp.logical_and(k == 0, jnp.logical_not(middle))
         waits = jnp.logical_and(k == 0, middle)
@@ -664,15 +686,15 @@
 
         @pl.when(jnp.logical_and(k < nz - 1, jnp.logical_not(waits)))
         def _():
-            remote(gown.at[m, g, p], r_z.at[m, g, slot], z_s.at[m, g, zz], z_r.at[m, g, slot], {"z": to}).start()
+            remote(gown.at[m, g, p], z_place(m, g, slot), z_s.at[m, g, zz], z_r.at[m, g, slot], {"z": to}).start()
 
         @pl.when(jnp.logical_and(k == jnp.where(m == 0, 1, nz - 2), middle))
         def _():
             far = target(0)
             f = part(far, xc)
-            arrived(r_z.at[m, g, z], z_r.at[m, g, z])
-            gown[m, g, f] = (gown[m, g, f].astype(F32) + r_z[m, g, z].astype(F32)).astype(BF)
-            remote(gown.at[m, g, f], r_z.at[m, g, z], z_s.at[m, g, far], z_r.at[m, g, z], {"z": far}).start()
+            arrived(z_place(m, g, z), z_r.at[m, g, z])
+            gown[m, g, f] += z_place(m, g, z)[...]
+            remote(gown.at[m, g, f], z_place(m, g, z), z_s.at[m, g, far], z_r.at[m, g, z], {"z": far}).start()
 
     outs = (qo_out, up_out, dn_out)
 
@@ -693,9 +715,9 @@
 
             @pl.when(direct)
             def _():
-                arrived(r_z.at[m, g, source], z_r.at[m, g, source])
-
-            total += jnp.where(direct, r_z[m, g, source].astype(F32), 0.0)
+                arrived(z_place(m, g, source), z_r.at[m, g, source])
+
+            total += jnp.where(direct, z_place(m, g, source)[...].astype(F32), 0.0)
 
         @pl.when(y == g)
         def _():
@@ -709,15 +731,22 @@
 
     def slope_grads(m, a, b, extra):
         def unit(q):
-            g = q % 2
-            t = 2 * g + jnp.where(q < 2, 1 - c, c)
-            dst = gown.at[jnp.where(q < 2, 0, m), g]
-            for k in range(0, D, GW):
-                dst[:, k : k + GW] = dot_tn(a[...], b[t, :, k : k + GW]).astype(BF)
-
-            @pl.when(q < 2)
+            g, own = (q // 2, q % 2) if m == 2 else (q % 2, q // 2)
+            t = 2 * g + jnp.where(own == 0, 1 - c, c)
+            dst = gown.at[jnp.where(own == 0, 0, m), g]
+            for k in range(D // GW):
+                cols = slice(k * GW, (k + 1) * GW)
+                dst[:, cols] = dot_tn(a[...], b[t, :, cols]).astype(BF)
+
+                if m == 2 and k:
+                    pl.when(own == 0)(core_piece(g, k - 1).start)
+
+            @pl.when(own == 0)
             def _():
-                core_send(m, g).start()
+                if m == 2:
+                    core_piece(g, D // GW - 1).start()
+                else:
+                    core_send(m, g).start()
 
         weave(4, unit, extra)
 
@@ -730,15 +759,18 @@
 
     def core_over(m):
         for g in range(2):
-            core_send(m, g).wait_send()
+            if m == 2:
+                for k in range(D // GW):
+                    core_piece(g, k).wait_send()
+            else:
+                core_send(m, g).wait_send()
 
     slope_grads(
         2,
         d_ffn,
         act,
         {
-            1: then((core_fetch, 2, 0)),
-            2: then((core_fetch, 2, 1), (core_add, 2, 0)),
+            1: then((core_add, 2, 0)),
             3: then((core_add, 2, 1), (core_over, 2)),
         },
     )
@@ -746,20 +778,20 @@
     def up_back(i):
         back_up(i // N_CHUNK, i % N_CHUNK, d_ffn, w, slope)
 
-    weave(GROUPS * N_CHUNK, up_back, {7: then((sum_event, 0)), 11: then((sum_event, 1))})
+    weave(GROUPS * N_CHUNK, up_back, {1: then((sum_event, 0)), 7: then((sum_event, 1)), 11: then((sum_event, 2))})
     for i in range(2):
         y_copy(i).wait()
     has_left(y_stage(2), e_s.at[0])
-    slope_grads(1, mid_low, slope, {1: then((sum_event, 2)), 3: then((sum_event, 3))})
+    slope_grads(1, mid_low, slope, {1: then((sum_event, 3)), 3: then((sum_event, 4))})
     for g in range(2):
-        core_fetch(1, g)
+        core_fetch(g)
     weave(
         N_CHUNK,
         lambda i: back_first_norm(i, slope, w, prm, mid, n1, s1, d_ffn, ngrad),
         {
             0: then((core_add, 1, 0), (core_add, 1, 1), (core_over, 1)),
-            1: then((sum_event, 4)),
-            2: then((sum_event, 5)),
+            1: then((sum_event, 5)),
+            2: then((sum_event, 6)),
         },
     )
 
@@ -776,7 +808,7 @@
 
     send_norms(0, start)
     loop(GROUPS, lambda t: back_heads(t, d_ffn, wo, slope))
-    sum_event(6)
+    sum_event(7)
     send_norms(0, recv)
     send_norms(0, lambda cp: cp.wait_send())
     n_c[...] += ngrad[...]
@@ -787,10 +819,10 @@
 
         @pl.when(i % 2 == 1)
         def _():
-            sum_event(7 + i // 2)
+            sum_event(8 + i // 2)
 
     loop(GROUPS * per, attention_back)
-    seen = 7 + GROUPS * per // 2
+    seen = 8 + GROUPS * per // 2
 
     def qkv_grads(q):
         g, own = q // 2, q % 2
@@ -817,9 +849,8 @@
         qkv_grads,
         {
             0: then((sum_event, seen)),
-            1: then((core_fetch, 0, 0), (sum_event, seen + 1)),
-            2: then((core_add, 0, 0), (sum_event, seen + 2)),
-            3: then((core_fetch, 0, 1), (core_add, 0, 1)),
+            1: then((core_add, 0, 0), (sum_event, seen + 1)),
+            3: then((core_add, 0, 1), (sum_event, seen + 2)),
         },
     )
     seen += 3
@@ -840,8 +871,8 @@
         def _():
             give_back(mid_low.at[pl.ds(0, EXT_ROWS)], g_back, 1, start)
 
-    weave(N_CHUNK, inputs_back, {1: then((sum_event, seen)), 2: then((sum_event, seen + 1))})
-    seen += 2
+    weave(N_CHUNK, inputs_back, {1: then((sum_event, seen))})
+    seen += 1
     after = 4 * nz
     if seen < after:
         loop(after - seen, lambda q: sum_event(seen + q))
@@ -905,9 +936,9 @@
         for zz in range(nz):
             @pl.when(z != zz)
             def _():
-                has_left(r_x.at[0, 0, 0], z_s.at[m, g, zz])
-
-            has_left(r_x.at[0, 0, 0], x_s.at[m, g, zz])
+                has_left(x_place(0, 0, 0), z_s.at[m, g, zz])
+
+            has_left(x_place(0, 0, 0), x_s.at[m, g, zz])
 
     loop(6, sums_sent)
     loop(6, gather_sent)
@@ -948,7 +979,7 @@
             out((2, 8, D), F32),
             out((OWN_ROWS, D), BF),
             out((OWN_ROWS, D), BF),
-            out((3, 2, D, D), BF),
+            out((2, D, D), BF),
         ),
         in_specs=[S, S] + [ANY] * 6 + [V, V],
         out_specs=(ANY, ANY, ANY, ANY, ANY, V, ANY, ANY, ANY),
@@ -967,8 +998,7 @@
             pltpu.VMEM((GROUPS, ROWS, D), BF),
             pltpu.VMEM((ROWS, D), BF),
             pltpu.VMEM((3, 2, D, D), BF),
-            pltpu.VMEM((3, 2, nz, rows, D), BF),
-            pltpu.VMEM((3, 2, nz, rows, D), BF),
+            pltpu.VMEM((2, 3, 2 * nz * rows, D), BF),
             pltpu.VMEM((3, rows, D), BF),
             pltpu.VMEM(qkv.shape, BF),
             pltpu.VMEM(wout.shape, BF),
@@ -988,6 +1018,7 @@
             sem((2, 2)), sem((2,)),
             sem((nz + 2,)), sem((nz + 2,)),
             sem((3, 2)), sem((3, 2)),
+            sem((2, 3)), sem((2, 3)),
             sem((3, 2, nz)), sem((3, 2, nz)),
             sem((3, 2, nz)), sem((3, 2, nz)),
             sem((3,)), sem((3,)),

time: 201 us -> 198 us (0.985)
  Pallas kernels: 200 us -> 197 us
    pallas_call x1, Pallas kernels: 194 us -> 192 us  [run_step(): pl.pallas_call(partial(step_kernel, nz, rows), out_shape=(out((OWN_ROWS,...]
where the time goes in v5:
time: 198 us
  Pallas kernels  197 us (99%)
    pallas_call x1, Pallas kernels, run_step(): pl.pallas_call(partial(step_kernel, nz, rows), out_shape=(out((OWN_ROWS,...  192 us
    pallas_call x1, Pallas kernels, deliver(): pl.pallas_call(partial(deliver_kernel, cols), out_shape=tuple((out(*p) fo...  5.29 us

profile of v5, /device:TPU:5, one launch (start us, length us, event | category | flops | bytes accessed | tf_op | source)
XLA Modules:
  0.0 197.7 jit_solution(3736053701938482715)
XLA Ops:
  0.6 191.6 %layer_step.1 = (bf16[640,768]{1,0:T(8,128)(2,1)}, f32[640,768]{1,0:T(8,128)}, f32[2,96,768]{2,1,0:T(8,128)}, f32[2,96,768]{2,1,0:T(8,128)}, f32[2,96,768]{2,1,0...) custom-call(s32[16]{0:T(128)} %tags.1, s32[16]{0:T(128)} %lens.1, ...), custom_call_target="tpu_custom_call" | custom-call | tf_op jit(solution)/shard_map/layer_step/pallas_call | solution.py:971
  192.3 5.3 %deliver.1 = (bf16[640,768]{1,0:T(8,128)(2,1)}, f32[640,768]{1,0:T(8,128)}, f32[2,3,96,192]{3,2,1,0:T(8,128)}, f32[2,96,192]{2,1,0:T(8,128)}, f32[2,96,768]{2,1,...) custom-call(bf16[640,768]{1,0:T(8,128)(2,1)} %get-tuple-element.22.y_in, ...), custom_call_target="tpu_custom_call" | custom-call | tf_op jit(solution)/shard_map/deliver/pallas_call | solution.py:1085

commit v6 on v5

--- a/solution.py
+++ b/solution.py
@@ -269,33 +269,34 @@
 
 MIXED = (2, 1)
 GATHER_FIRST = (
-    ('X', 0, 0), ('L', 0, 0), ('y', 0), ('X', 0, 1), ('L', 0, 1),
-    ('z', 0, 0, 1), ('z', 0, 1, 1), ('z', 0, 0, 2), ('x', 0, 0, 0), ('z', 0, 1, 2),
-    ('z', 0, 0, 3), ('y', 1), ('L', 1, 1), ('x', 0, 1, 1), ('z', 0, 1, 3),
-    ('x', 0, 1, 0), ('y', 2), ('X', 2, 1), ('L', 1, 0), ('X', 1, 0),
-    ('x', 0, 0, 2), ('X', 1, 1), ('z', 1, 1, 1), ('x', 0, 0, 3), ('L', 2, 0),
-    ('x', 0, 0, 1), ('x', 0, 1, 2), ('x', 0, 1, 3), ('z', 1, 0, 1),
+    ('X', 1, 0), ('L', 0, 0), ('y', 0), ('X', 0, 1), ('L', 0, 1),
+    ('z', 0, 0, 1), ('z', 0, 1, 1), ('y', 1), ('L', 1, 1), ('x', 0, 1, 0),
+    ('X', 0, 0), ('z', 0, 1, 2), ('x', 1, 0, 0), ('z', 0, 0, 2), ('x', 0, 1, 1),
+    ('x', 0, 0, 1), ('L', 1, 0), ('z', 0, 1, 3), ('z', 0, 0, 3), ('x', 0, 0, 0),
+    ('y', 2), ('X', 2, 1), ('x', 0, 1, 3), ('z', 1, 1, 1), ('x', 0, 1, 2),
+    ('z', 1, 0, 1), ('x', 0, 0, 2), ('L', 2, 0), ('x', 0, 0, 3), ('z', 1, 1, 2),
+    ('X', 1, 1),
 )
 GATHER_QKV = {
-    6: (('z', 1, 1, 2),),
-    11: (('z', 1, 0, 2),),
+    7: (('z', 1, 0, 2),),
+    10: (('x', 2, 1, 0),),
 }
 GATHER_ATTEND = {
-    2: (('x', 2, 1, 0),),
-    3: (('x', 1, 1, 1), ('x', 1, 0, 0), ('z', 1, 0, 3),),
-    4: (('L', 2, 1), ('z', 1, 1, 3), ('x', 1, 1, 0),),
-    5: (('z', 2, 0, 1), ('X', 2, 0),),
+    1: (('L', 2, 1), ('z', 1, 1, 3), ('z', 1, 0, 3), ('z', 2, 0, 1),),
+    2: (('X', 2, 0),),
+    5: (('x', 1, 1, 1), ('x', 1, 1, 2),),
+    6: (('z', 2, 1, 1), ('x', 1, 1, 0),),
+    7: (('z', 2, 0, 2), ('x', 1, 0, 1),),
 }
 GATHER_NORM = {
-    0: (('z', 2, 1, 1),),
-    1: (('x', 1, 0, 3), ('x', 1, 0, 1), ('x', 1, 1, 2), ('x', 1, 0, 2), ('x', 1, 1, 3),),
-    2: (('z', 2, 0, 2),),
+    0: (('x', 1, 0, 2), ('x', 1, 1, 3), ('x', 1, 0, 3),),
 }
 GATHER_UP = {
     3: (('z', 2, 1, 2),),
-    5: (('z', 2, 0, 3),),
-    8: (('x', 2, 0, 1),),
-    10: (('x', 2, 0, 0), ('x', 2, 0, 2), ('x', 2, 0, 3),),
+    4: (('z', 2, 0, 3),),
+    7: (('x', 2, 0, 1),),
+    9: (('x', 2, 0, 0),),
+    10: (('x', 2, 0, 3), ('x', 2, 0, 2),),
     11: (('z', 2, 1, 3),),
 }
 
@@ -880,6 +881,17 @@
         finish(2, g)
     loop(2, lambda q: sum_event(after + q))
 
+    def sums_sent(i):
+        m, g = i // 2, i % 2
+        for zz in range(nz):
+            @pl.when(z != zz)
+            def _():
+                has_left(x_place(0, 0, 0), z_s.at[m, g, zz])
+
+            has_left(x_place(0, 0, 0), x_s.at[m, g, zz])
+
+    loop(6, gather_sent)
+
     trips = [
         pltpu.make_async_copy(g_back, proj.at[0, pl.ds(0, OWN_ROWS)], io_s.at[0]),
         pltpu.make_async_copy(y_out, proj.at[1, pl.ds(0, OWN_ROWS)], io_s.at[1]),
@@ -916,6 +928,16 @@
     for g in range(2):
         finish(1, g)
     loop(nz - 1, lambda q: sum_event(after + nz + q))
+    g_copy.wait()
+
+    def widen(m):
+        arrived(oth.at[m], y_r.at[m])
+        out_stage(m, 1)[...] = oth[m].astype(F32)
+        out_copy(m, 1).start()
+
+    widen(2)
+    widen(1)
+    loop(4, lambda i: sums_sent(2 + i))
     total = n_x[...]
     for dz in range(1, nz):
         arrived(n_z.at[dz], ng_r.at[1 + dz])
@@ -925,23 +947,9 @@
     finish(0, 0)
     sum_event(after + 2 * nz - 1)
     finish(0, 1)
-    g_copy.wait()
-    for m in (2, 1, 0):
-        arrived(oth.at[m], y_r.at[m])
-        out_stage(m, 1)[...] = oth[m].astype(F32)
-        out_copy(m, 1).start()
-
-    def sums_sent(i):
-        m, g = i // 2, i % 2
-        for zz in range(nz):
-            @pl.when(z != zz)
-            def _():
-                has_left(x_place(0, 0, 0), z_s.at[m, g, zz])
-
-            has_left(x_place(0, 0, 0), x_s.at[m, g, zz])
-
-    loop(6, sums_sent)
-    loop(6, gather_sent)
+    widen(0)
+
+    loop(2, sums_sent)
     for g in range(2):
         core_send(0, g).wait_send()
     for m in range(3):
@@ -1057,19 +1065,22 @@
         gain_out[k] = turned[0:2, :cols]
         bias_out[k] = turned[2:4, :cols]
     first.wait()
-    for k in range(2):
+
+    def unpack(k):
         tail = []
         for i in range(3):
             v_qkv[k, i] = v_qo[k, :, GW * i : GW * i + GW - HEAD_DIM]
             tail.append(v_qo[k, :, GW * (i + 1) - HEAD_DIM : GW * (i + 1)])
         v_out[k] = jnp.concatenate(tail, 1)
-    stores.append(pltpu.make_async_copy(v_qkv, qkv_out, out_s.at[n]))
-    stores.append(pltpu.make_async_copy(v_out, wout_out, out_s.at[n + 1]))
+        for j, (src, dst) in enumerate(((v_qkv, qkv_out), (v_out, wout_out))):
+            stores.append(pltpu.make_async_copy(src.at[k], dst.at[k], out_s.at[n + 2 * k + j]))
+            stores[-1].start()
+
     for i in range(n):
         loads[i].wait()
         stores[i].start()
-    for cp in stores[n:]:
-        cp.start()
+        if i in (1, 3):
+            unpack(i // 2)
     for cp in stores:
         cp.wait()
 
@@ -1089,7 +1100,7 @@
         ),
         in_specs=[ANY] * 5 + [V],
         out_specs=(ANY,) * 6 + (V, V),
-        scratch_shapes=[pltpu.VMEM(*p) for p in whole + shapes] + [sem((9,)), sem((10,))],
+        scratch_shapes=[pltpu.VMEM(*p) for p in whole + shapes] + [sem((9,)), sem((12,))],
         name="deliver",
     )(y_in, g_in, qo, up_in, dn_in, sums)
 

time: 198 us -> 195 us (0.985)
  Pallas kernels: 197 us -> 194 us
    pallas_call x1, Pallas kernels: 192 us -> 189 us  [run_step(): pl.pallas_call(partial(step_kernel, nz, rows), out_shape=(out((OWN_ROWS,...]
where the time goes in v6:
time: 195 us
  Pallas kernels  194 us (99%)
    pallas_call x1, Pallas kernels, run_step(): pl.pallas_call(partial(step_kernel, nz, rows), out_shape=(out((OWN_ROWS,...  189 us
    pallas_call x1, Pallas kernels, deliver(): pl.pallas_call(partial(deliver_kernel, cols), out_shape=tuple((out(*p) fo...  5.06 us

profile of v6, /device:TPU:5, one launch (start us, length us, event | category | flops | bytes accessed | tf_op | source)
XLA Modules:
  0.0 194.8 jit_solution(13119256861940112774)
XLA Ops:
  0.6 188.9 %layer_step.1 = (bf16[640,768]{1,0:T(8,128)(2,1)}, f32[640,768]{1,0:T(8,128)}, f32[2,96,768]{2,1,0:T(8,128)}, f32[2,96,768]{2,1,0:T(8,128)}, f32[2,96,768]{2,1,0...) custom-call(s32[16]{0:T(128)} %tags.1, s32[16]{0:T(128)} %lens.1, ...), custom_call_target="tpu_custom_call" | custom-call | tf_op jit(solution)/shard_map/layer_step/pallas_call | solution.py:979
  189.5 5.1 %deliver.1 = (bf16[640,768]{1,0:T(8,128)(2,1)}, f32[640,768]{1,0:T(8,128)}, f32[2,3,96,192]{3,2,1,0:T(8,128)}, f32[2,96,192]{2,1,0:T(8,128)}, f32[2,96,768]{2,1,...) custom-call(bf16[640,768]{1,0:T(8,128)(2,1)} %get-tuple-element.22.y_in, ...), custom_call_target="tpu_custom_call" | custom-call | tf_op jit(solution)/shard_map/deliver/pallas_call | solution.py:1096

commit v7 on v6

--- a/solution.py
+++ b/solution.py
@@ -614,6 +614,10 @@
         y_copy(i).start()
     give_back(y_stage(2), y_back, 0, start)
 
+    def columns(g, other):
+        pair = jnp.where(g == 0, 1 - y, y)
+        return 2 * pair + jnp.where(other, 1 - c, c)
+
     def x_place(m, g, i):
         return r_xz.at[0, m, pl.ds(pl.multiple_of((g * nz + i) * rows, rows), rows)]
 
@@ -630,9 +634,14 @@
     def fetch(g):
         return pltpu.make_async_copy(r_c.at[g], act.at[2 * g + 1 - c, pl.ds(0, D)], stage_s.at[g])
 
-    def core_piece(g, k):
-        cols = pl.ds(k * GW, GW)
-        return remote(gown.at[0, g, :, cols], gown.at[1, g, :, cols], cp_s.at[g, k], cp_r.at[g, k], core)
+    half = D // 2
+
+    def half_rows(k):
+        return pl.ds(pl.multiple_of(half * jnp.where(z < nz // 2, 1 - k, k), half), half)
+
+    def core_half(g, k):
+        r = half_rows(k)
+        return remote(gown.at[0, g, r], gown.at[1, g, r], cp_s.at[g, k], cp_r.at[g, k], core)
 
     def core_fetch(g):
         arrived(r_c.at[g], c_r.at[1, g])
@@ -645,29 +654,30 @@
         up = jnp.where(k < z, k, k + 1)
         return jnp.where(k == nz - 1, z, jnp.where(z < nz // 2, down, up))
 
+    def add_and_cross(m, g, from_core, first, count):
+        def add(i):
+            p = part(target(first + i % count), lax.rem(xc + 1 + i // count, 2))
+            gown[m, g, p] += from_core[p]
+
+        def over(k):
+            zz = target(first + k)
+            remote(gown.at[m, g, part(zz, 1 - xc)], x_place(m, g, zz), x_s.at[m, g, zz], x_r.at[m, g, zz], other_x).start()
+
+        loop(count + 1, add)
+        loop(count, over)
+        loop(count - 1, lambda i: add(count + 1 + i))
+
     def core_add(m, g):
-        if m == 2:
-            for k in range(D // GW):
-                core_piece(g, k).wait_recv()
-            from_core = gown.at[1, g]
+        from_core = act.at[2 * g + 1 - c, pl.ds(0, D)]
+        if m == 1:
+            fetch(g).wait()
         else:
-            from_core = act.at[2 * g + 1 - c, pl.ds(0, D)]
-            if m == 1:
-                fetch(g).wait()
-            else:
-                arrived(from_core, c_r.at[0, g])
-
-        def add(i):
-            p = part(target(i % nz), lax.rem(xc + 1 + i // nz, 2))
-            gown[m, g, p] += from_core[p]
-
-        def over(k):
-            zz = target(k)
-            remote(gown.at[m, g, part(zz, 1 - xc)], x_place(m, g, zz), x_s.at[m, g, zz], x_r.at[m, g, zz], other_x).start()
-
-        loop(nz + 1, add)
-        loop(nz, over)
-        loop(nz - 1, lambda i: add(nz + 1 + i))
+            arrived(from_core, c_r.at[0, g])
+        add_and_cross(m, g, from_core, 0, nz)
+
+    def half_add(g, k):
+        core_half(g, k).wait_recv()
+        add_and_cross(2, g, gown.at[1, g], k * (nz // 2), nz // 2)
 
     def sum_event(q):
         m = 2 - q // (2 * nz)
@@ -679,23 +689,31 @@
         p = part(zz, xc)
         gown[m, g, p] += over[...]
 
-        joins = jnp.logical_and(k == 0, jnp.logical_not(middle))
-        waits = jnp.logical_and(k == 0, middle)
         beside = jnp.where(z == 0, 1, nz - 2)
+        joins = jnp.logical_and(k < 2, jnp.logical_not(middle))
         to = jnp.where(joins, beside, zz)
-        slot = jnp.where(joins, beside, z)
-
-        @pl.when(jnp.logical_and(k < nz - 1, jnp.logical_not(waits)))
+        slot = jnp.where(joins, jnp.where(k == 0, beside, nz - 1 - z), z)
+
+        @pl.when(jnp.logical_and(k < nz - 1, jnp.logical_or(k == nz - 2, jnp.logical_not(middle))))
         def _():
             remote(gown.at[m, g, p], z_place(m, g, slot), z_s.at[m, g, zz], z_r.at[m, g, slot], {"z": to}).start()
 
-        @pl.when(jnp.logical_and(k == jnp.where(m == 0, 1, nz - 2), middle))
+        def relay(k, slot):
+            to = target(k)
+            q = part(to, xc)
+            arrived(z_place(m, g, slot), z_r.at[m, g, slot])
+            gown[m, g, q] += z_place(m, g, slot)[...]
+            remote(gown.at[m, g, q], z_place(m, g, z), z_s.at[m, g, to], z_r.at[m, g, z], {"z": to}).start()
+
+        early = jnp.where(m == 0, 1, 0)
+
+        @pl.when(jnp.logical_and(k == nz - 2 - early, middle))
         def _():
-            far = target(0)
-            f = part(far, xc)
-            arrived(z_place(m, g, z), z_r.at[m, g, z])
-            gown[m, g, f] += z_place(m, g, z)[...]
-            remote(gown.at[m, g, f], z_place(m, g, z), z_s.at[m, g, far], z_r.at[m, g, z], {"z": far}).start()
+            relay(0, z)
+
+        @pl.when(jnp.logical_and(k == nz - 1 - early, middle))
+        def _():
+            relay(1, jnp.where(z == 1, nz - 1, 0))
 
     outs = (qo_out, up_out, dn_out)
 
@@ -712,7 +730,7 @@
         total = gown[m, g, part(z, xc)].astype(F32)
         for dz in range(1, nz):
             source = z_of(dz)
-            direct = jnp.abs(source - z) < nz - 1
+            direct = jnp.abs(source - z) <= jnp.where(middle, 1, 2)
 
             @pl.when(direct)
             def _():
@@ -720,36 +738,41 @@
 
             total += jnp.where(direct, z_place(m, g, source)[...].astype(F32), 0.0)
 
-        @pl.when(y == g)
-        def _():
+        if g == 1:
             out_stage(m, 0)[...] = total
             out_copy(m, 0).start()
-
-        @pl.when(y != g)
-        def _():
+        else:
             mid_low[EXT_ROWS + m * rows : EXT_ROWS + (m + 1) * rows] = total.astype(BF)
             last_send(m).start()
 
-    def slope_grads(m, a, b, extra):
+    def up_grads(extra):
         def unit(q):
-            g, own = (q // 2, q % 2) if m == 2 else (q % 2, q // 2)
-            t = 2 * g + jnp.where(own == 0, 1 - c, c)
-            dst = gown.at[jnp.where(own == 0, 0, m), g]
-            for k in range(D // GW):
-                cols = slice(k * GW, (k + 1) * GW)
-                dst[:, cols] = dot_tn(a[...], b[t, :, cols]).astype(BF)
-
-                if m == 2 and k:
-                    pl.when(own == 0)(core_piece(g, k - 1).start)
+            g, own = q % 2, q // 2
+            t = columns(g, own == 0)
+            dst = gown.at[own, g]
+            for k in range(0, D, GW):
+                dst[:, k : k + GW] = dot_tn(mid_low[...], slope[t, :, k : k + GW]).astype(BF)
 
             @pl.when(own == 0)
             def _():
-                if m == 2:
-                    core_piece(g, D // GW - 1).start()
-                else:
-                    core_send(m, g).start()
+                core_send(1, g).start()
 
         weave(4, unit, extra)
+
+    def down_grads(extra):
+        def unit(q):
+            g, k, own = q // 4, (q // 2) % 2, q % 2
+            t = columns(g, own == 0)
+            r = half_rows(k)
+            dst = gown.at[2 * own, g, r]
+            for j in range(0, D, GW):
+                dst[:, j : j + GW] = dot_tn(d_ffn[:, r], act[t, :, j : j + GW]).astype(BF)
+
+            @pl.when(own == 0)
+            def _():
+                core_half(g, k).start()
+
+        weave(8, unit, extra)
 
     def then(*steps):
         def run():
@@ -761,29 +784,28 @@
     def core_over(m):
         for g in range(2):
             if m == 2:
-                for k in range(D // GW):
-                    core_piece(g, k).wait_send()
+                for k in range(2):
+                    core_half(g, k).wait_send()
             else:
                 core_send(m, g).wait_send()
 
-    slope_grads(
-        2,
-        d_ffn,
-        act,
+    down_grads(
         {
-            1: then((core_add, 2, 0)),
-            3: then((core_add, 2, 1), (core_over, 2)),
-        },
+            2: then((half_add, 0, 0)),
+            3: then((half_add, 0, 1)),
+            5: then((half_add, 1, 0)),
+            7: then((half_add, 1, 1), (core_over, 2)),
+        }
     )
 
     def up_back(i):
         back_up(i // N_CHUNK, i % N_CHUNK, d_ffn, w, slope)
 
-    weave(GROUPS * N_CHUNK, up_back, {1: then((sum_event, 0)), 7: then((sum_event, 1)), 11: then((sum_event, 2))})
+    weave(GROUPS * N_CHUNK, up_back, {0: then((sum_event, 0)), 5: then((sum_event, 1)), 10: then((sum_event, 2))})
     for i in range(2):
         y_copy(i).wait()
     has_left(y_stage(2), e_s.at[0])
-    slope_grads(1, mid_low, slope, {1: then((sum_event, 3)), 3: then((sum_event, 4))})
+    up_grads({1: then((sum_event, 3)), 3: then((sum_event, 4))})
     for g in range(2):
         core_fetch(g)
     weave(
@@ -839,7 +861,7 @@
             def _():
                 gown[0, g, :, col : col + 128] = value
 
-        grad_qkv_out(2 * g + jnp.where(own == 0, 1 - c, c), x, proj, d_ffn, hout, store)
+        grad_qkv_out(columns(g, own == 0), x, proj, d_ffn, hout, store)
 
         @pl.when(own == 0)
         def _():
@@ -946,8 +968,8 @@
     send_norms(3, start)
     finish(0, 0)
     sum_event(after + 2 * nz - 1)
+    widen(0)
     finish(0, 1)
-    widen(0)
 
     loop(2, sums_sent)
     for g in range(2):
@@ -1026,7 +1048,7 @@
             sem((2, 2)), sem((2,)),
             sem((nz + 2,)), sem((nz + 2,)),
             sem((3, 2)), sem((3, 2)),
-            sem((2, 3)), sem((2, 3)),
+            sem((2, 2)), sem((2, 2)),
             sem((3, 2, nz)), sem((3, 2, nz)),
             sem((3, 2, nz)), sem((3, 2, nz)),
             sem((3,)), sem((3,)),

time: 195 us -> 193 us (0.990)
  Pallas kernels: 194 us -> 190 us
    pallas_call x1, Pallas kernels: 189 us -> 185 us  [run_step(): pl.pallas_call(partial(step_kernel, nz, rows), out_shape=(out((OWN_ROWS,...]
where the time goes in v7:
time: 193 us; the launch traced here: 191 us
  Pallas kernels  190 us (98%)
    pallas_call x1, Pallas kernels, run_step(): pl.pallas_call(partial(step_kernel, nz, rows), out_shape=(out((OWN_ROWS,...  185 us
    pallas_call x1, Pallas kernels, deliver(): pl.pallas_call(partial(deliver_kernel, cols), out_shape=tuple((out(*p) fo...  5.06 us

profile of v7, /device:TPU:5, one launch (start us, length us, event | category | flops | bytes accessed | tf_op | source)
XLA Modules:
  0.0 190.9 jit_solution(17531511511196781469)
XLA Ops:
  0.6 185.0 %layer_step.1 = (bf16[640,768]{1,0:T(8,128)(2,1)}, f32[640,768]{1,0:T(8,128)}, f32[2,96,768]{2,1,0:T(8,128)}, f32[2,96,768]{2,1,0:T(8,128)}, f32[2,96,768]{2,1,0...) custom-call(s32[16]{0:T(128)} %tags.1, s32[16]{0:T(128)} %lens.1, ...), custom_call_target="tpu_custom_call" | custom-call | tf_op jit(solution)/shard_map/layer_step/pallas_call | solution.py:1001
  185.7 5.1 %deliver.1 = (bf16[640,768]{1,0:T(8,128)(2,1)}, f32[640,768]{1,0:T(8,128)}, f32[2,3,96,192]{3,2,1,0:T(8,128)}, f32[2,96,192]{2,1,0:T(8,128)}, f32[2,96,768]{2,1,...) custom-call(bf16[640,768]{1,0:T(8,128)(2,1)} %get-tuple-element.22.y_in, ...), custom_call_target="tpu_custom_call" | custom-call | tf_op jit(solution)/shard_map/deliver/pallas_call | solution.py:1118

commit v8 on v7

--- a/solution.py
+++ b/solution.py
@@ -901,7 +901,7 @@
         loop(after - seen, lambda q: sum_event(seen + q))
     for g in range(2):
         finish(2, g)
-    loop(2, lambda q: sum_event(after + q))
+    loop(nz, lambda q: sum_event(after + q))
 
     def sums_sent(i):
         m, g = i // 2, i % 2
@@ -942,7 +942,6 @@
         y_again.start()
 
     g_copy.start()
-    loop(nz - 2, lambda q: sum_event(after + 2 + q))
     send_norms(1, recv)
     send_norms(1, lambda cp: cp.wait_send())
     n_x[...] += n_c[...]

time: 193 us -> 192 us (level)
  no operation moved by 1% of the time
where the time goes in v8:
time: 192 us; the launch traced here: 190 us
  Pallas kernels  189 us (98%)
    pallas_call x1, Pallas kernels, run_step(): pl.pallas_call(partial(step_kernel, nz, rows), out_shape=(out((OWN_ROWS,...  184 us
    pallas_call x1, Pallas kernels, deliver(): pl.pallas_call(partial(deliver_kernel, cols), out_shape=tuple((out(*p) fo...  5.06 us

profile of v8, /device:TPU:5, one launch (start us, length us, event | category | flops | bytes accessed | tf_op | source)
XLA Modules:
  0.0 190.0 jit_solution(8952969866563172533)
XLA Ops:
  0.6 184.1 %layer_step.1 = (bf16[640,768]{1,0:T(8,128)(2,1)}, f32[640,768]{1,0:T(8,128)}, f32[2,96,768]{2,1,0:T(8,128)}, f32[2,96,768]{2,1,0:T(8,128)}, f32[2,96,768]{2,1,0...) custom-call(s32[16]{0:T(128)} %tags.1, s32[16]{0:T(128)} %lens.1, ...), custom_call_target="tpu_custom_call" | custom-call | tf_op jit(solution)/shard_map/layer_step/pallas_call | solution.py:1000
  184.8 5.1 %deliver.1 = (bf16[640,768]{1,0:T(8,128)(2,1)}, f32[640,768]{1,0:T(8,128)}, f32[2,3,96,192]{3,2,1,0:T(8,128)}, f32[2,96,192]{2,1,0:T(8,128)}, f32[2,96,768]{2,1,...) custom-call(bf16[640,768]{1,0:T(8,128)(2,1)} %get-tuple-element.22.y_in, ...), custom_call_target="tpu_custom_call" | custom-call | tf_op jit(solution)/shard_map/deliver/pallas_call | solution.py:1117

commit v9 on v8

--- a/solution.py
+++ b/solution.py
@@ -794,14 +794,14 @@
             2: then((half_add, 0, 0)),
             3: then((half_add, 0, 1)),
             5: then((half_add, 1, 0)),
-            7: then((half_add, 1, 1), (core_over, 2)),
+            7: then((half_add, 1, 1), (sum_event, 0), (core_over, 2)),
         }
     )
 
     def up_back(i):
         back_up(i // N_CHUNK, i % N_CHUNK, d_ffn, w, slope)
 
-    weave(GROUPS * N_CHUNK, up_back, {0: then((sum_event, 0)), 5: then((sum_event, 1)), 10: then((sum_event, 2))})
+    weave(GROUPS * N_CHUNK, up_back, {4: then((sum_event, 1)), 9: then((sum_event, 2))})
     for i in range(2):
         y_copy(i).wait()
     has_left(y_stage(2), e_s.at[0])

time: 192 us -> 192 us (level)
  no operation moved by 1% of the time
where the time goes in v9:
time: 192 us; the launch traced here: 190 us
  Pallas kernels  189 us (98%)
    pallas_call x1, Pallas kernels, run_step(): pl.pallas_call(partial(step_kernel, nz, rows), out_shape=(out((OWN_ROWS,...  184 us
    pallas_call x1, Pallas kernels, deliver(): pl.pallas_call(partial(deliver_kernel, cols), out_shape=tuple((out(*p) fo...  5.06 us

profile of v9, /device:TPU:5, one launch (start us, length us, event | category | flops | bytes accessed | tf_op | source)
XLA Modules:
  0.0 189.9 jit_solution(7734154151673843677)
XLA Ops:
  0.6 184.0 %layer_step.1 = (bf16[640,768]{1,0:T(8,128)(2,1)}, f32[640,768]{1,0:T(8,128)}, f32[2,96,768]{2,1,0:T(8,128)}, f32[2,96,768]{2,1,0:T(8,128)}, f32[2,96,768]{2,1,0...) custom-call(s32[16]{0:T(128)} %tags.1, s32[16]{0:T(128)} %lens.1, ...), custom_call_target="tpu_custom_call" | custom-call | tf_op jit(solution)/shard_map/layer_step/pallas_call | solution.py:1000
  184.6 5.1 %deliver.1 = (bf16[640,768]{1,0:T(8,128)(2,1)}, f32[640,768]{1,0:T(8,128)}, f32[2,3,96,192]{3,2,1,0:T(8,128)}, f32[2,96,192]{2,1,0:T(8,128)}, f32[2,96,768]{2,1,...) custom-call(bf16[640,768]{1,0:T(8,128)(2,1)} %get-tuple-element.22.y_in, ...), custom_call_target="tpu_custom_call" | custom-call | tf_op jit(solution)/shard_map/deliver/pallas_call | solution.py:1117
